TPU v7x, 32 devices: a whole 2x2x4 slice. The times are simulated.
32 devices in a mesh: shard: 4 (over x, core), rep: 8 (over z, y).
Axes of the slice: x: 2, y: 2, z: 4, core: 2. Of those that a mesh axis runs over, the one named last changes fastest.
Arguments:
- tokens: bfloat16 [2, 32, 1024, 768], P(None, ('shard', 'rep')), may hold values from -6 to 6
- segment_ids: int32 [2, 32, 1024], P(None, ('shard', 'rep')), may hold values from 0 to 7, never falling along the last dimension, each value on 1 to 512 neighbouring positions
- cotangent: bfloat16 [2, 32, 1024, 768], P(None, ('shard', 'rep')), may hold values from -6 to 6
- w_qkv: bfloat16 [768, 2304], P('shard'), may hold values from -0.21875 to 0.21875
- b_query: bfloat16 [768], P('shard'), may hold values from -1.75 to 1.75
- b_value: bfloat16 [768], P('shard'), may hold values from -1.75 to 1.75
- w_out: bfloat16 [768, 768], P('shard'), may hold values from -0.875 to 0.875
- b_out: bfloat16 [768], P('shard'), may hold values from -1.75 to 1.75
- gain_one: bfloat16 [768], P('shard'), may hold values from 0.25 to 1.75
- shift_one: bfloat16 [768], P('shard'), may hold values from -1.75 to 1.75
- w_in: bfloat16 [768, 3072], P('shard'), may hold values from -0.21875 to 0.21875
- b_in: bfloat16 [3072], P('shard'), may hold values from -1.75 to 1.75
- w_ffo: bfloat16 [3072, 768], P('shard'), may hold values from -0.109375 to 0.109375
- b_ffo: bfloat16 [768], P('shard'), may hold values from -1.75 to 1.75
- gain_two: bfloat16 [768], P('shard'), may hold values from 0.25 to 1.75
- shift_two: bfloat16 [768], P('shard'), may hold values from -1.75 to 1.75
Outputs:
- layer_output: bfloat16 [2, 32, 1024, 768], P(None, ('shard', 'rep'))
- input_grad: bfloat16 [2, 32, 1024, 768], P(None, ('shard', 'rep'))
- grad_qkv: float32 [768, 2304], P('shard')
- grad_query_bias: float32 [768], P('shard')
- grad_value_bias: float32 [768], P('shard')
- grad_out_proj: float32 [768, 768], P('shard')
- grad_out_bias: float32 [768], P('shard')
- grad_gain_one: float32 [768], P('shard')
- grad_shift_one: float32 [768], P('shard')
- grad_in_proj: float32 [768, 3072], P('shard')
- grad_in_bias: float32 [3072], P('shard')
- grad_ffo_proj: float32 [3072, 768], P('shard')
- grad_ffo_bias: float32 [768], P('shard')
- grad_gain_two: float32 [768], P('shard')
- grad_shift_two: float32 [768], P('shard')
Inputs may be any that keep to these rules, and one draw needn't show every extreme that they name: `segment_ids`: along each sequence the ids never fall; each of the 8 documents has 1 to 512 tokens, and a document of exactly 512 tokens occurs.
All inputs are finite; a program needn't handle non-finite values.
Results may differ from a plain program's by a relative error of at most 0.02.
Values may be sent and summed in bfloat16 or wider, within the bound.
A program may use at most 320 MiB of HBM per device.

v0:
```python
import math

import jax
import jax.numpy as jnp
from jax import lax
from jax.sharding import PartitionSpec as P

HEADS = 12
HEAD_DIM = 64


epsilon = 1e-05
masked_score = -1e30


def for_sending(shard):
    return jax.tree.map(lambda a: a.astype(jnp.bfloat16) if a.dtype == jnp.float32 else a, shard)


def outer_sum(left, right):
    return lax.dot_general(
        left, right, (((0,), (0,)), ((), ())), preferred_element_type=jnp.float32
    )


def back_product(grad, weight):
    return lax.dot_general(
        grad, weight, (((1,), (1,)), ((), ())), preferred_element_type=jnp.float32
    )


def layer_norm(values, gain_vec, shift_vec):
    center = values - jnp.mean(values, axis=-1, keepdims=True)
    spread = jnp.mean(center * center, axis=-1, keepdims=True)
    rstd_rows = lax.rsqrt(spread + epsilon)
    scaled = center * rstd_rows
    return (scaled * gain_vec + shift_vec, scaled, rstd_rows)


def norm_backward(grad, scaled, rstd_rows, gain_vec):
    inner = grad * gain_vec
    d_input = rstd_rows * (
        inner
        - jnp.mean(inner, axis=-1, keepdims=True)
        - scaled * jnp.mean(inner * scaled, axis=-1, keepdims=True)
    )
    return (d_input, jnp.sum(grad * scaled, axis=0), jnp.sum(grad, axis=0))


def gelu_slope(values):
    return 0.5 * (1.0 + lax.erf(values * (1.0 / math.sqrt(2.0)))) + values * jnp.exp(
        -0.5 * values * values
    ) * (1.0 / math.sqrt(2.0 * math.pi))


def block_scores(queries, key_rows, query_segment, key_segment, scale):
    scores = (
        jnp.einsum("qhd,khd->hqk", queries, key_rows, preferred_element_type=jnp.float32) * scale
    )
    same_doc = query_segment[:, None] == key_segment[None, :]
    return jnp.where(same_doc[None], scores, masked_score)


def attend_sequence(joined, segment, block_rows, scale):
    queries = joined[:, 0]
    key_rows = joined[:, 1]
    value_rows = joined[:, 2]
    length = joined.shape[0]
    blocks = length // block_rows
    query_blocks = queries.reshape((blocks, block_rows) + queries.shape[1:])
    segment_blocks = segment.reshape(blocks, block_rows)

    def one_block(packed):
        query_part, segment_part = packed
        scores = block_scores(query_part, key_rows, segment_part, segment, scale)
        row_top = jnp.max(scores, axis=-1, keepdims=True)
        exponent = jnp.exp(scores - row_top)
        total = jnp.sum(exponent, axis=-1, keepdims=True)
        probs_low = (exponent / total).astype(jnp.bfloat16)
        result = jnp.einsum(
            "hqk,khd->qhd", probs_low, value_rows, preferred_element_type=jnp.float32
        )
        return (result.astype(jnp.bfloat16), (row_top + jnp.log(total))[..., 0])

    outputs, log_total = lax.map(one_block, (query_blocks, segment_blocks))
    return (outputs.reshape(queries.shape), log_total)


def attend_backward(joined, segment, grad_out, log_total, block_rows, scale):
    queries = joined[:, 0]
    key_rows = joined[:, 1]
    value_rows = joined[:, 2]
    length = joined.shape[0]
    blocks = length // block_rows
    query_blocks = queries.reshape((blocks, block_rows) + queries.shape[1:])
    segment_blocks = segment.reshape(blocks, block_rows)
    grad_blocks = grad_out.reshape((blocks, block_rows) + grad_out.shape[1:])

    def one_block(carry, packed):
        key_grad, value_grad = carry
        query_part, segment_part, grad_part, lse_part = packed
        scores = block_scores(query_part, key_rows, segment_part, segment, scale)
        probs = jnp.exp(scores - lse_part[..., None])
        d_probs = jnp.einsum(
            "qhd,khd->hqk", grad_part, value_rows, preferred_element_type=jnp.float32
        )
        row_dot = jnp.sum(probs * d_probs, axis=-1, keepdims=True)
        d_scores = (probs * (d_probs - row_dot)).astype(jnp.bfloat16)
        query_grad = (
            jnp.einsum("hqk,khd->qhd", d_scores, key_rows, preferred_element_type=jnp.float32)
            * scale
        )
        key_grad = (
            key_grad
            + jnp.einsum("hqk,qhd->khd", d_scores, query_part, preferred_element_type=jnp.float32)
            * scale
        )
        value_grad = value_grad + jnp.einsum(
            "hqk,qhd->khd",
            probs.astype(jnp.bfloat16),
            grad_part,
            preferred_element_type=jnp.float32,
        )
        return ((key_grad, value_grad), query_grad)

    zeros_start = jnp.zeros(key_rows.shape, jnp.float32)
    (key_grad, value_grad), query_grads = lax.scan(
        one_block,
        (zeros_start, zeros_start),
        (query_blocks, segment_blocks, grad_blocks, log_total),
    )
    return jnp.stack([query_grads.reshape(key_rows.shape), key_grad, value_grad], axis=1)


def forward_pass(full, tokens_mb, segment_mb):
    (
        w_qkv,
        b_query,
        b_value,
        w_out,
        b_out,
        gain_one,
        shift_one,
        w_in,
        b_in,
        w_ffo,
        b_ffo,
        gain_two,
        shift_two,
    ) = full
    rows, model_width = tokens_mb.shape
    sequences, length = segment_mb.shape
    bias_all = jnp.concatenate([b_query, jnp.zeros_like(b_query), b_value]).astype(jnp.float32)
    projected = (jnp.dot(tokens_mb, w_qkv, preferred_element_type=jnp.float32) + bias_all).astype(
        jnp.bfloat16
    )
    joined = projected.reshape(sequences, length, 3, HEADS, HEAD_DIM)
    scale = 1.0 / math.sqrt(HEAD_DIM)
    block_rows = min(512, length)
    attended, log_total = lax.map(
        lambda packed: attend_sequence(packed[0], packed[1], block_rows, scale),
        (joined, segment_mb),
    )
    attended = attended.reshape(rows, model_width)
    branch = jnp.dot(attended, w_out, preferred_element_type=jnp.float32) + b_out.astype(
        jnp.float32
    )
    normed_one, scaled_one, rstd_one = layer_norm(
        tokens_mb.astype(jnp.float32) + branch,
        gain_one.astype(jnp.float32),
        shift_one.astype(jnp.float32),
    )
    normed_low = normed_one.astype(jnp.bfloat16)
    ffn_pre = jnp.dot(normed_low, w_in, preferred_element_type=jnp.float32) + b_in.astype(
        jnp.float32
    )
    hidden = jax.nn.gelu(ffn_pre, approximate=False).astype(jnp.bfloat16)
    second = jnp.dot(hidden, w_ffo, preferred_element_type=jnp.float32) + b_ffo.astype(jnp.float32)
    output, scaled_two, rstd_two = layer_norm(
        normed_low.astype(jnp.float32) + second,
        gain_two.astype(jnp.float32),
        shift_two.astype(jnp.float32),
    )
    kept = (
        joined,
        log_total,
        attended,
        scaled_one,
        rstd_one,
        normed_low,
        ffn_pre,
        hidden,
        scaled_two,
        rstd_two,
    )
    return (output.astype(jnp.bfloat16), kept)


def backward_pass(full, tokens_mb, segment_mb, kept, cotangent_mb):
    (
        w_qkv,
        b_query,
        b_value,
        w_out,
        b_out,
        gain_one,
        shift_one,
        w_in,
        b_in,
        w_ffo,
        b_ffo,
        gain_two,
        shift_two,
    ) = full
    (
        joined,
        log_total,
        attended,
        scaled_one,
        rstd_one,
        normed_low,
        ffn_pre,
        hidden,
        scaled_two,
        rstd_two,
    ) = kept
    rows, model_width = tokens_mb.shape
    sequences, length = segment_mb.shape
    d_res_two, d_gain_two, d_shift_two = norm_backward(
        cotangent_mb.astype(jnp.float32), scaled_two, rstd_two, gain_two.astype(jnp.float32)
    )
    d_second = d_res_two.astype(jnp.bfloat16)
    d_ffo_bias = jnp.sum(d_second.astype(jnp.float32), axis=0)
    d_ffo_proj = outer_sum(hidden, d_second)
    d_pre = (back_product(d_second, w_ffo) * gelu_slope(ffn_pre)).astype(jnp.bfloat16)
    d_in_bias = jnp.sum(d_pre.astype(jnp.float32), axis=0)
    d_in_proj = outer_sum(normed_low, d_pre)
    d_norm_one = d_res_two + back_product(d_pre, w_in)
    d_res_one, d_gain_one, d_shift_one = norm_backward(
        d_norm_one, scaled_one, rstd_one, gain_one.astype(jnp.float32)
    )
    d_branch = d_res_one.astype(jnp.bfloat16)
    d_out_bias = jnp.sum(d_branch.astype(jnp.float32), axis=0)
    d_out_proj = outer_sum(attended, d_branch)
    d_attended = (
        back_product(d_branch, w_out)
        .astype(jnp.bfloat16)
        .reshape(sequences, length, HEADS, HEAD_DIM)
    )
    scale = 1.0 / math.sqrt(HEAD_DIM)
    block_rows = min(512, length)
    d_joined = lax.map(
        lambda packed: attend_backward(
            packed[0], packed[1], packed[2], packed[3], block_rows, scale
        ),
        (joined, segment_mb, d_attended, log_total),
    )
    d_projected = d_joined.reshape(rows, 3 * model_width).astype(jnp.bfloat16)
    projected_sums = jnp.sum(d_projected.astype(jnp.float32), axis=0)
    d_query_bias = projected_sums[:model_width]
    d_value_bias = projected_sums[2 * model_width :]
    d_qkv_proj = outer_sum(tokens_mb, d_projected)
    d_tokens = (d_res_one + back_product(d_projected, w_qkv)).astype(jnp.bfloat16)
    gradients = (
        d_qkv_proj,
        d_query_bias,
        d_value_bias,
        d_out_proj,
        d_out_bias,
        d_gain_one,
        d_shift_one,
        d_in_proj,
        d_in_bias,
        d_ffo_proj,
        d_ffo_bias,
        d_gain_two,
        d_shift_two,
    )
    return (gradients, d_tokens)


def local(
    tokens,
    segment_ids,
    cotangent,
    w_qkv,
    b_query,
    b_value,
    w_out,
    b_out,
    gain_one,
    shift_one,
    w_in,
    b_in,
    w_ffo,
    b_ffo,
    gain_two,
    shift_two,
):
    shards = (
        w_qkv,
        b_query,
        b_value,
        w_out,
        b_out,
        gain_one,
        shift_one,
        w_in,
        b_in,
        w_ffo,
        b_ffo,
        gain_two,
        shift_two,
    )
    group_size = lax.axis_size("shard")
    micro_count, sequences, length, model_width = tokens.shape
    rows = sequences * length
    summed_local = tuple(
        (
            jnp.zeros((entry.shape[0] * group_size,) + entry.shape[1:], jnp.float32)
            for entry in shards
        )
    )
    owned = tuple((jnp.zeros(entry.shape, jnp.float32) for entry in shards))
    outputs = []
    token_grads = []
    for batch_index in range(micro_count):
        tokens_mb = tokens[batch_index].reshape(rows, model_width)
        segment_mb = segment_ids[batch_index]
        full = (
            lax.all_gather(shards[0], "shard", axis=0, tiled=True),
            lax.all_gather(shards[1], "shard", axis=0, tiled=True),
            lax.all_gather(shards[2], "shard", axis=0, tiled=True),
            lax.all_gather(shards[3], "shard", axis=0, tiled=True),
            lax.all_gather(shards[4], "shard", axis=0, tiled=True),
            lax.all_gather(shards[5], "shard", axis=0, tiled=True),
            lax.all_gather(shards[6], "shard", axis=0, tiled=True),
            lax.all_gather(shards[7], "shard", axis=0, tiled=True),
            lax.all_gather(shards[8], "shard", axis=0, tiled=True),
            lax.all_gather(shards[9], "shard", axis=0, tiled=True),
            lax.all_gather(shards[10], "shard", axis=0, tiled=True),
            lax.all_gather(shards[11], "shard", axis=0, tiled=True),
            lax.all_gather(shards[12], "shard", axis=0, tiled=True),
        )
        output, kept = forward_pass(full, tokens_mb, segment_mb)
        outputs.append(output.reshape(sequences, length, model_width))
        back_full = (
            lax.all_gather(shards[0], "shard", axis=0, tiled=True),
            lax.all_gather(shards[1], "shard", axis=0, tiled=True),
            lax.all_gather(shards[2], "shard", axis=0, tiled=True),
            lax.all_gather(shards[3], "shard", axis=0, tiled=True),
            lax.all_gather(shards[4], "shard", axis=0, tiled=True),
            lax.all_gather(shards[5], "shard", axis=0, tiled=True),
            lax.all_gather(shards[6], "shard", axis=0, tiled=True),
            lax.all_gather(shards[7], "shard", axis=0, tiled=True),
            lax.all_gather(shards[8], "shard", axis=0, tiled=True),
            lax.all_gather(shards[9], "shard", axis=0, tiled=True),
            lax.all_gather(shards[10], "shard", axis=0, tiled=True),
            lax.all_gather(shards[11], "shard", axis=0, tiled=True),
            lax.all_gather(shards[12], "shard", axis=0, tiled=True),
        )
        cotangent_mb = cotangent[batch_index].reshape(rows, model_width)
        gradients, d_tokens = backward_pass(back_full, tokens_mb, segment_mb, kept, cotangent_mb)
        token_grads.append(d_tokens.reshape(sequences, length, model_width))
        summed_local = jax.tree.map(jnp.add, summed_local, gradients)
    owned = jax.tree.map(
        lambda part: part.astype(jnp.float32),
        lax.psum_scatter(for_sending(summed_local), "shard", scatter_dimension=0, tiled=True),
    )
    totals = jax.tree.map(
        lambda part: part.astype(jnp.float32), lax.psum(for_sending(owned), "rep")
    )
    layer_output = jnp.stack(outputs, axis=0)
    input_grad = jnp.stack(token_grads, axis=0)
    return (
        layer_output,
        input_grad,
        totals[0],
        totals[1],
        totals[2],
        totals[3],
        totals[4],
        totals[5],
        totals[6],
        totals[7],
        totals[8],
        totals[9],
        totals[10],
        totals[11],
        totals[12],
    )


def solution(mesh):
    return jax.shard_map(
        local,
        mesh=mesh,
        in_specs=(
            P(None, ("shard", "rep"), None, None),
            P(None, ("shard", "rep"), None),
            P(None, ("shard", "rep"), None, None),
            P("shard", None),
            P("shard"),
            P("shard"),
            P("shard", None),
            P("shard"),
            P("shard"),
            P("shard"),
            P("shard", None),
            P("shard"),
            P("shard", None),
            P("shard"),
            P("shard"),
            P("shard"),
        ),
        out_specs=(
            P(None, ("shard", "rep"), None, None),
            P(None, ("shard", "rep"), None, None),
            P("shard", None),
            P("shard"),
            P("shard"),
            P("shard", None),
            P("shard"),
            P("shard"),
            P("shard"),
            P("shard", None),
            P("shard"),
            P("shard", None),
            P("shard"),
            P("shard"),
            P("shard"),
        ),
        check_vma=False,
    )
```

profile of v0, /device:TPU:0, one launch (start us, length us, event | category | flops | bytes accessed | tf_op | source)
XLA Modules:
  0.0 1266.4 jit_solution(4292303455172534214)
XLA Ops:
  72.7 71.1 %while.91 = (s32[]{:T(128)}, bf16[2,512,12,64]{1,3,2,0:T(8,128)(2,1)}, f32[2,12,512]{2,1,0:T(8,128)S(1)}, s32[2,512]{1,0:T(2,128)S(1)}, s32[1024]{0:T(1024)S(1)}...) while((s32[]{:T(128)}, ...), condition=%wide.region_11.12_spmd, body=%wide.region_8.11_spmd.sunk | while | flops 1687021568 | bytes 189500048 | solution.py:85
  178.4 70.2 %while.90 = (s32[]{:T(128)}, bf16[2,512,12,64]{1,3,2,0:T(8,128)(2,1)}, f32[2,12,512]{2,1,0:T(8,128)S(1)}, s32[2,512]{1,0:T(2,128)S(1)}, s32[1024]{0:T(1024)S(1)}...) while((s32[]{:T(128)}, ...), condition=%wide.region_3.4_spmd, body=%wide.region_0.3_spmd.sunk | while | flops 1687021568 | bytes 189500048 | solution.py:85
  272.2 67.3 %fusion.70 = (bf16[1024,3072]{1,0:T(8,128)(2,1)}, bf16[1024,3072]{1,0:T(8,128)(2,1)}, f32[1024,3072]{1,0:T(8,128)}) fusion(f32[3072]{0:T(1024)S(1)} %bitcast.357, f32[1024,3072]{1,0:T(8,128)S(1)} %fusion.150, bf16[1024,768]{0,1:T(8,128)(2,1)S(1)} %get-tuple-element.668, bf16[768,3072]{1,0:T(8,128)(2,1)S(1)} %copy-done.37), kind=kOutput, calls=%fused_computation.98 | convolution fusion | flops 5247074304 | bytes 44052480 | tf_op jit(solution)/shard_map/dot_general | solution.py:174
  362.8 15.9 %convert_reduce_fusion.1 = (f32[3072]{0:T(1024)}, bf16[1024,3072]{1,0:T(8,128)(2,1)}) fusion(f32[1024,3072]{1,0:T(8,128)} %get-tuple-element.685, f32[3072]{0:T(1024)S(1)} %bitcast.358, bf16[1024,768]{0,1:T(8,128)(2,1)S(1)} %get-tuple-element.635, bf16[3072,768]{1,0:T(8,128)(2,1)} %all-gather.12.cloned.1.call-done), kind=kOutput, calls=%fused_computation.115 | convolution fusion | flops 4872729600 | bytes 25190400 | tf_op jit(solution)/shard_map/dot_general | solution.py:27
  406.4 14.5 %convert_reduce_fusion.9 = (f32[768]{0:T(1024)}, f32[1024,768]{0,1:T(8,128)S(1)}, f32[768]{0:T(1024)}, f32[1024]{0:T(1024)S(1)}, f32[1024]{0:T(1024)S(1)}, /*index=5*/f32[768]{0:T(1024)}, f32[1024,768]{0,1:T(8,128)}) fusion(f32[1024]{0:T(1024)S(1)} %broadcast_multiply_fusion.4, f32[1024,768]{0,1:T(8,128)} %copy-done.30, f32[1024]{0:T(1024)S(1)} %copy-done.91, ...), kind=kOutput, calls=%fused_computation.185 | convolution fusion | flops 4853853184 | bytes 31521792 | tf_op jit(solution)/shard_map/dot_general | solution.py:27
  429.7 227.9 %while.92 = (s32[]{:T(128)}, f32[1024,12,64]{0,2,1:T(8,128)}, f32[1024,12,64]{0,2,1:T(8,128)}, bf16[2,512,12,64]{1,0,3,2:T(2,128)(2,1)}, bf16[2,512,12,64]{1,3,2...) while((s32[]{:T(128)}, f32[1024,12,64]{0,2,1:T(8,128)}, ...), condition=%wide.region_22.23_spmd.clone, body=%wide.region_20.22_spmd.clone.sunk | while | flops 4126140416 | bytes 225898224 | solution.py:127
  441.7 18.2 %multiply_reduce_fusion.14 = (f32[12,512]{1,0:T(8,128)S(1)}, f32[12,512,1024]{2,1,0:T(8,128)}) fusion(f32[12,512,1024]{2,1,0:T(8,128)} %fusion.256, f32[12,512]{1,0:T(8,128)S(1)} %dynamic-slice_bitcast_fusion.4, pred[512,1024]{1,0:T(8,128)(4,1)S(1)} %broadcast_compare_fusion.10, bf16[1024,12,64]{0,2,1:T(8,128)(2,1)} %get-tuple-element.1077, ...), kind=kOutput, calls=%fused_computation.37.clone.1 | convolution fusion | flops 836757504 | bytes 53264896 | tf_op jit(solution)/shard_map/while/body/eval_jaxpr/while/body/eval_jaxpr/qhd,khd->hqk/dot_general | solution.py:104
  460.0 21.3 %multiply_convert_fusion.4 = bf16[12,512,1024]{2,1,0:T(8,128)(2,1)} fusion(f32[12,512,1024]{2,1,0:T(8,128)} %get-tuple-element.933, f32[12,512,1024]{2,1,0:T(8,128)} %fusion.256, f32[12,512]{1,0:T(8,128)S(1)} %get-tuple-element.934, f32[12,512]{1,0:T(8,128)S(1)} %dynamic-slice_bitcast_fusion.4, pred[512,1024]{1,0:T(8,128)(4,1)S(1)} %broadcast_compare_fusion.10), kind=kLoop, calls=%fused_computation.36.clone.1 | loop fusion | flops 37748736 | bytes 63488000 | tf_op jit(solution)/shard_map/while/body/eval_jaxpr/while/body/eval_jaxpr/convert_element_type | solution.py:108
  493.2 27.1 %dynamic_update_slice.52 = bf16[2,512,12,64]{1,0,3,2:T(2,128)(2,1)} dynamic-update-slice(bf16[2,512,12,64]{1,0,3,2:T(2,128)(2,1)} %get-tuple-element.1057, bf16[1,512,12,64]{1,0,3,2:T(2,128)(2,1)S(1)} %copy.156, s32[]{:T(128)} %get-tuple-element.1054, s32[]{:T(128)} %constant.139.clone.1..sunk, s32[]{:T(128)} %constant.139.clone.1..sunk, s32[]{:T(128)} %constant.139.clone.1..sunk) | dynamic-update-slice | bytes 1572868 | tf_op jit(solution)/shard_map/while/body/eval_jaxpr/while/body/jit(dynamic_update_index_in_dim)/dynamic_update_slice | solution.py:127
  554.5 18.2 %multiply_reduce_fusion.14 = (f32[12,512]{1,0:T(8,128)S(1)}, f32[12,512,1024]{2,1,0:T(8,128)}) fusion(f32[12,512,1024]{2,1,0:T(8,128)} %fusion.256, f32[12,512]{1,0:T(8,128)S(1)} %dynamic-slice_bitcast_fusion.4, pred[512,1024]{1,0:T(8,128)(4,1)S(1)} %broadcast_compare_fusion.10, bf16[1024,12,64]{0,2,1:T(8,128)(2,1)} %get-tuple-element.1077, ...), kind=kOutput, calls=%fused_computation.37.clone.1 | convolution fusion | flops 836757504 | bytes 53264896 | tf_op jit(solution)/shard_map/while/body/eval_jaxpr/while/body/eval_jaxpr/qhd,khd->hqk/dot_general | solution.py:104
  572.7 21.3 %multiply_convert_fusion.4 = bf16[12,512,1024]{2,1,0:T(8,128)(2,1)} fusion(f32[12,512,1024]{2,1,0:T(8,128)} %get-tuple-element.933, f32[12,512,1024]{2,1,0:T(8,128)} %fusion.256, f32[12,512]{1,0:T(8,128)S(1)} %get-tuple-element.934, f32[12,512]{1,0:T(8,128)S(1)} %dynamic-slice_bitcast_fusion.4, pred[512,1024]{1,0:T(8,128)(4,1)S(1)} %broadcast_compare_fusion.10), kind=kLoop, calls=%fused_computation.36.clone.1 | loop fusion | flops 37748736 | bytes 63488000 | tf_op jit(solution)/shard_map/while/body/eval_jaxpr/while/body/eval_jaxpr/convert_element_type | solution.py:108
  606.0 27.1 %dynamic_update_slice.52 = bf16[2,512,12,64]{1,0,3,2:T(2,128)(2,1)} dynamic-update-slice(bf16[2,512,12,64]{1,0,3,2:T(2,128)(2,1)} %get-tuple-element.1057, bf16[1,512,12,64]{1,0,3,2:T(2,128)(2,1)S(1)} %copy.156, s32[]{:T(128)} %get-tuple-element.1054, s32[]{:T(128)} %constant.139.clone.1..sunk, s32[]{:T(128)} %constant.139.clone.1..sunk, s32[]{:T(128)} %constant.139.clone.1..sunk) | dynamic-update-slice | bytes 1572868 | tf_op jit(solution)/shard_map/while/body/eval_jaxpr/while/body/jit(dynamic_update_index_in_dim)/dynamic_update_slice | solution.py:127
  682.7 227.7 %while.93 = (s32[]{:T(128)}, f32[1024,12,64]{0,2,1:T(8,128)}, f32[1024,12,64]{0,2,1:T(8,128)}, bf16[2,512,12,64]{1,0,3,2:T(2,128)(2,1)}, bf16[2,512,12,64]{1,3,2...) while((s32[]{:T(128)}, f32[1024,12,64]{0,2,1:T(8,128)}, ...), condition=%wide.region_29.30_spmd.clone, body=%wide.region_27.29_spmd.clone.sunk | while | flops 4126140416 | bytes 225898224 | solution.py:127
  694.6 18.2 %multiply_reduce_fusion.15 = (f32[12,512]{1,0:T(8,128)S(1)}, f32[12,512,1024]{2,1,0:T(8,128)}) fusion(f32[12,512,1024]{2,1,0:T(8,128)} %fusion.266, f32[12,512]{1,0:T(8,128)S(1)} %dynamic-slice_bitcast_fusion.5, pred[512,1024]{1,0:T(8,128)(4,1)S(1)} %broadcast_compare_fusion.11, bf16[1024,12,64]{0,2,1:T(8,128)(2,1)} %get-tuple-element.1038, ...), kind=kOutput, calls=%fused_computation.65.clone.1 | convolution fusion | flops 836757504 | bytes 53264896 | tf_op jit(solution)/shard_map/while/body/eval_jaxpr/while/body/eval_jaxpr/qhd,khd->hqk/dot_general | solution.py:104
  712.9 21.3 %multiply_convert_fusion.5 = bf16[12,512,1024]{2,1,0:T(8,128)(2,1)} fusion(f32[12,512,1024]{2,1,0:T(8,128)} %get-tuple-element.946, f32[12,512,1024]{2,1,0:T(8,128)} %fusion.266, f32[12,512]{1,0:T(8,128)S(1)} %get-tuple-element.947, f32[12,512]{1,0:T(8,128)S(1)} %dynamic-slice_bitcast_fusion.5, pred[512,1024]{1,0:T(8,128)(4,1)S(1)} %broadcast_compare_fusion.11), kind=kLoop, calls=%fused_computation.64.clone.1 | loop fusion | flops 37748736 | bytes 63488000 | tf_op jit(solution)/shard_map/while/body/eval_jaxpr/while/body/eval_jaxpr/convert_element_type | solution.py:108
  746.1 27.1 %dynamic_update_slice.53 = bf16[2,512,12,64]{1,0,3,2:T(2,128)(2,1)} dynamic-update-slice(bf16[2,512,12,64]{1,0,3,2:T(2,128)(2,1)} %get-tuple-element.1018, bf16[1,512,12,64]{1,0,3,2:T(2,128)(2,1)S(1)} %copy.157, s32[]{:T(128)} %get-tuple-element.1015, s32[]{:T(128)} %constant.139.clone.1..sunk.1, s32[]{:T(128)} %constant.139.clone.1..sunk.1, s32[]{:T(128)} %constant.139.clone.1..sunk.1) | dynamic-update-slice | bytes 1572868 | tf_op jit(solution)/shard_map/while/body/eval_jaxpr/while/body/jit(dynamic_update_index_in_dim)/dynamic_update_slice | solution.py:127
  807.3 18.2 %multiply_reduce_fusion.15 = (f32[12,512]{1,0:T(8,128)S(1)}, f32[12,512,1024]{2,1,0:T(8,128)}) fusion(f32[12,512,1024]{2,1,0:T(8,128)} %fusion.266, f32[12,512]{1,0:T(8,128)S(1)} %dynamic-slice_bitcast_fusion.5, pred[512,1024]{1,0:T(8,128)(4,1)S(1)} %broadcast_compare_fusion.11, bf16[1024,12,64]{0,2,1:T(8,128)(2,1)} %get-tuple-element.1038, ...), kind=kOutput, calls=%fused_computation.65.clone.1 | convolution fusion | flops 836757504 | bytes 53264896 | tf_op jit(solution)/shard_map/while/body/eval_jaxpr/while/body/eval_jaxpr/qhd,khd->hqk/dot_general | solution.py:104
  825.6 21.3 %multiply_convert_fusion.5 = bf16[12,512,1024]{2,1,0:T(8,128)(2,1)} fusion(f32[12,512,1024]{2,1,0:T(8,128)} %get-tuple-element.946, f32[12,512,1024]{2,1,0:T(8,128)} %fusion.266, f32[12,512]{1,0:T(8,128)S(1)} %get-tuple-element.947, f32[12,512]{1,0:T(8,128)S(1)} %dynamic-slice_bitcast_fusion.5, pred[512,1024]{1,0:T(8,128)(4,1)S(1)} %broadcast_compare_fusion.11), kind=kLoop, calls=%fused_computation.64.clone.1 | loop fusion | flops 37748736 | bytes 63488000 | tf_op jit(solution)/shard_map/while/body/eval_jaxpr/while/body/eval_jaxpr/convert_element_type | solution.py:108
  858.8 27.1 %dynamic_update_slice.53 = bf16[2,512,12,64]{1,0,3,2:T(2,128)(2,1)} dynamic-update-slice(bf16[2,512,12,64]{1,0,3,2:T(2,128)(2,1)} %get-tuple-element.1018, bf16[1,512,12,64]{1,0,3,2:T(2,128)(2,1)S(1)} %copy.157, s32[]{:T(128)} %get-tuple-element.1015, s32[]{:T(128)} %constant.139.clone.1..sunk.1, s32[]{:T(128)} %constant.139.clone.1..sunk.1, s32[]{:T(128)} %constant.139.clone.1..sunk.1) | dynamic-update-slice | bytes 1572868 | tf_op jit(solution)/shard_map/while/body/eval_jaxpr/while/body/jit(dynamic_update_index_in_dim)/dynamic_update_slice | solution.py:127
  978.1 21.0 %reduce-scatter.7.cloned.1.call-done = bf16[192,768]{1,0:T(8,128)(2,1)} async-done(((bf16[768,768]{1,0:T(8,128)(2,1)}), bf16[192,768]{1,0:T(8,128)(2,1)}) %reduce-scatter.7.cloned.1.call-update) | async-done | bytes 294928 | tf_op jit(solution)/shard_map/reduce_scatter | solution.py:368
  999.2 50.6 %reduce-scatter.11.cloned.1.call-done = bf16[768,768]{1,0:T(8,128)(2,1)} async-done(((bf16[3072,768]{1,0:T(8,128)(2,1)}), bf16[768,768]{1,0:T(8,128)(2,1)}) %reduce-scatter.11.cloned.1.call-update) | async-done | bytes 1179664 | tf_op jit(solution)/shard_map/reduce_scatter | solution.py:368
  1049.7 50.5 %reduce-scatter.9.cloned.1.call-done = bf16[192,3072]{1,0:T(8,128)(2,1)} async-done(((bf16[768,3072]{1,0:T(8,128)(2,1)}), bf16[192,3072]{1,0:T(8,128)(2,1)}) %reduce-scatter.9.cloned.1.call-update) | async-done | bytes 1179664 | tf_op jit(solution)/shard_map/reduce_scatter | solution.py:368
  1111.5 23.4 %all-reduce.17 = (bf16[192]{0:T(256)(128)(2,1)S(1)}, bf16[192]{0:T(256)(128)(2,1)S(1)}, bf16[192]{0:T(256)(128)(2,1)S(1)}, bf16[192]{0:T(256)(128)(2,1)S(1)}, bf...) all-reduce(bf16[192]{0:T(256)(128)(2,1)S(1)} %dynamic-slice.11, ...), channel_id=1, replica_groups=mesh['shard'=4,'rep'=8] {'rep'}, use_global_device_ids=true, to_apply=%region_35.36 | all-reduce | flops 2304 | bytes 9216 | tf_op jit(solution)/shard_map/psum | solution.py:371
  1164.9 87.7 %all-reduce.23.cloned.1.call-done = (bf16[192,2304]{0,1:T(8,128)(2,1)}, bf16[192,768]{1,0:T(8,128)(2,1)}, bf16[192,3072]{1,0:T(8,128)(2,1)}, bf16[768,768]{1,0:T(8,128)(2,1)}) async-done(((bf16[192,2304]{0,1:T(8,128)(2,1)}, bf16[192,768]{1,0:T(8,128)(2,1)}, bf16[192,3072]{1,0:T(8,128)(2,1)}, bf16[768,768]{1,0:T(8,128)(2,1)}), (bf16[192,2304]{0,1:T(8,128)(2,1)}, bf16[192,768]{1,0:T(8,128)(2,1)}, ...) | async-done | bytes 3538960 | tf_op jit(solution)/shard_map/psum | solution.py:371
  (543 shorter events, 649.0 us)
Async XLA Ops:
  7.3 40.4 %all-gather.6.cloned.1.call-start = ((), (), s32[]{:S(2)}) async-start(), calls=%async_computation.4 | async-start | bytes 4423680 | tf_op jit(solution)/shard_map/all_gather | solution.py:331
  8.0 141.6 %all-gather.8.cloned.1.call-start = ((), (), s32[]{:S(2)}) async-start(), calls=%async_computation.5 | async-start | bytes 1474560 | tf_op jit(solution)/shard_map/all_gather | solution.py:334
  8.8 250.4 %all-gather.10.cloned.1.call-start = ((), (), s32[]{:S(2)}) async-start(), calls=%async_computation.6 | async-start | bytes 5898240 | tf_op jit(solution)/shard_map/all_gather | solution.py:338
  9.5 330.0 %all-gather.12.cloned.1.call-start = ((), (), s32[]{:S(2)}) async-start(), calls=%async_computation.7 | async-start | bytes 5898240 | tf_op jit(solution)/shard_map/all_gather | solution.py:340
  10.1 965.7 %reduce-scatter.13.cloned.1.call-start = ((), (), s32[]{:S(2)}) async-start(), calls=%async_computation.11 | async-start | bytes 4423680
  259.1 90.4 %copy-start.50 = (bf16[1024,768]{0,1:T(8,128)(2,1)}, bf16[1024,768]{0,1:T(8,128)(2,1)S(1)}, u32[]{:S(2)}) copy-start(bf16[1024,768]{0,1:T(8,128)(2,1)S(1)} %get-tuple-element.668) | copy-start | bytes 4718596
  272.2 67.3 %copy-start.33 = (bf16[1024,768]{0,1:T(8,128)(2,1)S(1)}, bf16[1024,768]{0,1:T(8,128)(2,1)}, u32[]{:S(2)}) copy-start(bf16[1024,768]{0,1:T(8,128)(2,1)} %copy-done.32) | copy-start | bytes 4718596
  272.2 67.3 %copy-start.108 = (f32[768]{0:T(1024)S(1)}, f32[768]{0:T(1024)}, u32[]{:S(2)}) copy-start(f32[768]{0:T(1024)} %convert_element_type.325) | copy-start | bytes 9220
  349.1 57.2 %copy-start.16 = (f32[1024,768]{0,1:T(8,128)}, f32[1024,768]{0,1:T(8,128)S(1)}, u32[]{:S(2)}) copy-start(f32[1024,768]{0,1:T(8,128)S(1)} %get-tuple-element.689) | copy-start | bytes 9437188
  349.1 57.2 %copy-start.70 = (f32[1024]{0:T(1024)}, f32[1024]{0:T(1024)S(1)}, u32[]{:S(2)}) copy-start(f32[1024]{0:T(1024)S(1)} %broadcast_multiply_fusion.8) | copy-start | bytes 12292
  349.5 56.8 %copy-start.76 = (f32[1024]{0:T(1024)}, f32[1024]{0:T(1024)S(1)}, u32[]{:S(2)}) copy-start(f32[1024]{0:T(1024)S(1)} %add_rsqrt_fusion) | copy-start | bytes 12292
  362.8 30.5 %slice-start = ((s8[12582912]{0:T(1024)(128)(4,1)}), s8[4194304]{0:T(1024)(128)(4,1)S(1)}, s32[]{:S(2)}) async-start(s8[12582912]{0:T(1024)(128)(4,1)} %bitcast.336), calls=%async_computation.13 | async-start | bytes 8388608
  362.8 30.5 %slice-start.1 = ((s8[12582912]{0:T(1024)(128)(4,1)}), s8[4194304]{0:T(1024)(128)(4,1)S(1)}, s32[]{:S(2)}) async-start(s8[12582912]{0:T(1024)(128)(4,1)} %bitcast.336), calls=%async_computation.14 | async-start | bytes 8388608
  929.6 69.6 %reduce-scatter.7.cloned.1.call-start = ((), (), s32[]{:S(2)}) async-start(), calls=%async_computation.8 | async-start | bytes 1474560 | tf_op jit(solution)/shard_map/reduce_scatter | solution.py:368
  936.1 113.6 %reduce-scatter.11.cloned.1.call-start = ((), (), s32[]{:S(2)}) async-start(), calls=%async_computation.10 | async-start | bytes 5898240 | tf_op jit(solution)/shard_map/reduce_scatter | solution.py:368
  955.0 145.3 %reduce-scatter.9.cloned.1.call-start = ((), (), s32[]{:S(2)}) async-start(), calls=%async_computation.9 | async-start | bytes 5898240 | tf_op jit(solution)/shard_map/reduce_scatter | solution.py:368
  973.3 279.4 %all-reduce.23.cloned.1.call-start = ((), (), s32[]{:S(2)}) async-start(), calls=%async_computation.12 | async-start | bytes 7667712 | tf_op jit(solution)/shard_map/psum | solution.py:371
  975.6 124.7 %copy-start.111 = (f32[768]{0:T(1024)S(1)}, f32[768]{0:T(1024)}, u32[]{:S(2)}) copy-start(f32[768]{0:T(1024)} %get-tuple-element.512) | copy-start | bytes 9220
  975.6 124.7 %copy-start.113 = (f32[768]{0:T(1024)S(1)}, f32[768]{0:T(1024)}, u32[]{:S(2)}) copy-start(f32[768]{0:T(1024)} %get-tuple-element.675) | copy-start | bytes 9220
  975.6 124.9 %copy-start.96 = (f32[768]{0:T(1024)S(1)}, f32[768]{0:T(1024)}, u32[]{:S(2)}) copy-start(f32[768]{0:T(1024)} %get-tuple-element.636) | copy-start | bytes 9220
  975.6 124.9 %copy-start.112 = (f32[768]{0:T(1024)S(1)}, f32[768]{0:T(1024)}, u32[]{:S(2)}) copy-start(f32[768]{0:T(1024)} %get-tuple-element.638) | copy-start | bytes 9220
  975.6 124.9 %copy-start.105 = (f32[3072]{0:T(1024)S(1)}, f32[3072]{0:T(1024)}, u32[]{:S(2)}) copy-start(f32[3072]{0:T(1024)} %get-tuple-element.692) | copy-start | bytes 36868
  975.6 124.9 %copy-start.106 = (f32[3072]{0:T(1024)S(1)}, f32[3072]{0:T(1024)}, u32[]{:S(2)}) copy-start(f32[3072]{0:T(1024)} %get-tuple-element.694) | copy-start | bytes 36868
  1100.3 48.0 %slice-start.3 = ((s8[4718592]{0:T(1024)(128)(4,1)}), s8[524288]{0:T(1024)(128)(4,1)S(1)}, s32[]{:S(2)}) async-start(s8[4718592]{0:T(1024)(128)(4,1)} %bitcast.343), calls=%async_computation.16 | async-start | bytes 1048576
  (137 other events, 1021.2 us)
Sparse Core Ops, SparseCore 0:
  9.6 33.6 all-gather.5
  44.9 17.4 all-gather.7
  63.9 37.4 all-gather.9
  102.8 37.4 all-gather.11
  929.7 40.8 reduce-scatter.12
  973.5 25.6 reduce-scatter.6
  1001.7 47.9 reduce-scatter.10
  1052.3 47.9 reduce-scatter.8
  1104.9 147.7 all-reduce.22
where the time goes:
time: 1280 us; the launch traced here: 1270 us
  matrix products  560 us (44%)
  local copies, waits for them, and re-layouts  243 us (19%)
  waiting for transfers between devices  213 us (17%)
  other arithmetic  178 us (14%)
  blocking collectives  52.7 us (4%)
  between operations  18 us (1%)
    reduce_scatter x3, waiting for transfers between devices, local(): lax.psum_scatter(for_sending(summed_local), 'shard', scatter_dimension=0,...  122 us
    dynamic_update_slice x8, local copies, waits for them, and re-layouts, attend_backward(): lax.scan(one_block, (zeros_start, zeros_start), (query_blocks, segment_bl...  119 us
    dot_general x8, matrix products, block_scores(): jnp.einsum('qhd,khd->hqk', queries, key_rows, preferred_element_type=jnp....  88.5 us
    psum x1, waiting for transfers between devices, local(): lax.psum(for_sending(owned), 'rep')  87.7 us
    convert_element_type x4, other arithmetic, one_block(): d_scores = (probs * (d_probs - row_dot)).astype(jnp.bfloat16)  85.2 us
    dot_general x2, matrix products, forward_pass(): jnp.dot(normed_low, w_in, preferred_element_type=jnp.float32)  75.7 us
    dot_general x4, matrix products, one_block(): jnp.einsum('qhd,khd->hqk', grad_part, value_rows, preferred_element_type=...  73 us
    dot_general x8, matrix products, back_product(): lax.dot_general(grad, weight, (((1,), (1,)), ((), ())), preferred_element...  71.1 us
  transfers between devices with their start and end apart: 9, of which 4 were waited for; matrix products, arithmetic and copies ran while one was open for 29% of the time, Pallas kernels for 0%

commit v1 on v0

v1 whole, which is shorter than its diff:
```python
import functools
import math

import jax
import jax.numpy as jnp
from jax import lax
from jax.experimental import pallas as pl
from jax.experimental.pallas import tpu as pltpu
from jax.sharding import PartitionSpec as P

HEADS = 12
HEAD_DIM = 64
PAIR = 2 * HEAD_DIM
TILE = 128

epsilon = 1e-05
masked_score = -1e30
BF = jnp.bfloat16
F32 = jnp.float32
VMEM_LIMIT = 60 * 2**20


def dot_nn(a, b):
    return lax.dot_general(a, b, (((1,), (0,)), ((), ())), preferred_element_type=F32)


def dot_nt(a, b):
    return lax.dot_general(a, b, (((1,), (1,)), ((), ())), preferred_element_type=F32)


def dot_tn(a, b):
    return lax.dot_general(a, b, (((0,), (0,)), ((), ())), preferred_element_type=F32)


def head_rows(value):
    lane = lax.broadcasted_iota(jnp.int32, (1, PAIR), 1)
    first = jnp.where(lane < HEAD_DIM, value, 0.0).astype(BF)
    second = jnp.where(lane < HEAD_DIM, 0.0, value).astype(BF)
    return first, second


def stack_heads(block, rows):
    return jnp.concatenate([block * rows[0], block * rows[1]], axis=0)


def diagonal_back(transposed):
    kept = jnp.concatenate(
        [transposed[:HEAD_DIM, :TILE], transposed[HEAD_DIM:, TILE:]], axis=0
    )
    return kept.T


def for_windows(count, tiles, body):
    sizes = [t for t in range(1, tiles + 1) if t < 7 or t == tiles]
    below = 0
    for size in sizes:
        @pl.when((count > below) & (count <= size))
        def _(size=size):
            body(size)

        below = size


def attend_forward_kernel(pairs, tiles, low_ref, count_ref, q_ref, k_ref, v_ref, kseg_ref, qseg_ref, o_ref, lse_ref):
    place = pl.program_id(0) * tiles + pl.program_id(1)
    low = low_ref[place]
    count = count_ref[place]
    rows_of = head_rows(1.0 / math.sqrt(HEAD_DIM))

    def window(size):
        start = jnp.minimum(low, tiles - size) * TILE
        chunks = [pl.ds(pl.multiple_of(start + c * TILE, TILE), TILE) for c in range(size)]
        whole = pl.ds(pl.multiple_of(start, TILE), size * TILE)
        masks = [kseg_ref[c, :] == qseg_ref[0] for c in chunks]
        for p in range(pairs):
            lanes = slice(p * PAIR, (p + 1) * PAIR)
            queries = stack_heads(q_ref[:, lanes], rows_of)
            scores = []
            for c, mask in zip(chunks, masks):
                part = dot_nt(k_ref[c, lanes], queries)
                scores.append(
                    jnp.concatenate(
                        [
                            jnp.where(mask, part[:, :TILE], masked_score),
                            jnp.where(mask, part[:, TILE:], masked_score),
                        ],
                        axis=1,
                    )
                )
            top = functools.reduce(jnp.maximum, [jnp.max(s, axis=0, keepdims=True) for s in scores])
            exps = [jnp.exp(s - top) for s in scores]
            total = functools.reduce(jnp.add, [jnp.sum(e, axis=0, keepdims=True) for e in exps])
            weights = jnp.concatenate([e.astype(BF) for e in exps], axis=0)
            mixed = dot_tn(v_ref[whole, lanes], weights) / total
            o_ref[:, lanes] = diagonal_back(mixed).astype(BF)
            lse_ref[0, p : p + 1, :] = top + jnp.log(total)

    for_windows(count, tiles, window)


def attend_backward_kernel(
    pairs, tiles, low_ref, count_ref, q_ref, k_ref, v_ref, do_ref, o_ref, lse_ref, kseg_ref, qseg_ref,
    dq_ref, dk_ref, dv_ref, dk_acc, dv_acc,
):
    group = pl.program_id(1)
    block = pl.program_id(2)
    place = pl.program_id(0) * tiles + block
    low = low_ref[place]
    count = count_ref[place]
    scale = 1.0 / math.sqrt(HEAD_DIM)
    scaled_rows = head_rows(scale)
    plain_rows = head_rows(1.0)

    @pl.when(block == 0)
    def _():
        dk_acc[...] = jnp.zeros_like(dk_acc)
        dv_acc[...] = jnp.zeros_like(dv_acc)

    def window(size):
        start = jnp.minimum(low, tiles - size) * TILE
        chunks = [pl.ds(pl.multiple_of(start + c * TILE, TILE), TILE) for c in range(size)]
        whole = pl.ds(pl.multiple_of(start, TILE), size * TILE)
        masks = [kseg_ref[c, :] == qseg_ref[0] for c in chunks]
        for p in range(pairs):
            lanes = slice(p * PAIR, (p + 1) * PAIR)
            queries = stack_heads(q_ref[:, lanes], scaled_rows)
            grads = do_ref[:, lanes]
            stacked = stack_heads(grads, plain_rows)
            product = (grads.astype(F32) * o_ref[:, lanes].astype(F32)).T
            row_dot = jnp.concatenate(
                [
                    jnp.sum(product[:HEAD_DIM], axis=0, keepdims=True),
                    jnp.sum(product[HEAD_DIM:], axis=0, keepdims=True),
                ],
                axis=1,
            )
            lse = lse_ref[0, pl.ds(group * pairs + p, 1), :]
            kept = []
            for c, mask in zip(chunks, masks):
                part = dot_nt(k_ref[c, lanes], queries) - lse
                d_probs = dot_nt(v_ref[c, lanes], stacked)
                probs = jnp.exp(
                    jnp.concatenate(
                        [
                            jnp.where(mask, part[:, :TILE], masked_score),
                            jnp.where(mask, part[:, TILE:], masked_score),
                        ],
                        axis=1,
                    )
                )
                d_scores = (probs * (d_probs - row_dot)).astype(BF)
                kept.append(d_scores)
                dv_acc[c, lanes] += dot_nn(probs.astype(BF), stacked)
                dk_acc[c, lanes] += dot_nn(d_scores, queries)
            mixed = dot_tn(k_ref[whole, lanes], jnp.concatenate(kept, axis=0)) * scale
            dq_ref[:, lanes] = diagonal_back(mixed).astype(BF)

    for_windows(count, tiles, window)

    @pl.when(block == tiles - 1)
    def _():
        dk_ref[...] = dk_acc[...].astype(BF)
        dv_ref[...] = dv_acc[...].astype(BF)


def windows_of(segments):
    sequences, length = segments.shape
    tiles = length // TILE
    blocked = segments.reshape(sequences, tiles, TILE)
    first = blocked[:, :, 0]
    last = blocked[:, :, TILE - 1]
    starts = jnp.sum((segments[:, None, :] < first[:, :, None]).astype(jnp.int32), axis=-1)
    ends = jnp.sum((segments[:, None, :] <= last[:, :, None]).astype(jnp.int32), axis=-1)
    low = starts // TILE
    count = (ends + TILE - 1) // TILE - low
    key_ids = jnp.broadcast_to(segments.reshape(sequences * length, 1), (sequences * length, TILE))
    query_ids = blocked.reshape(sequences * tiles, 1, TILE)
    return low.reshape(-1), count.reshape(-1), key_ids, query_ids


def attend_forward(projected, windows, sequences):
    low, count, key_ids, query_ids = windows
    rows = projected.shape[0]
    width = projected.shape[1] // 3
    length = rows // sequences
    tiles = length // TILE
    pairs = width // PAIR
    return pl.pallas_call(
        functools.partial(attend_forward_kernel, pairs, tiles),
        grid_spec=pltpu.PrefetchScalarGridSpec(
            num_scalar_prefetch=2,
            grid=(sequences, tiles),
            in_specs=[
                pl.BlockSpec((TILE, width), lambda s, b, *_: (s * tiles + b, 0)),
                pl.BlockSpec((length, width), lambda s, b, *_: (s, 1)),
                pl.BlockSpec((length, width), lambda s, b, *_: (s, 2)),
                pl.BlockSpec((length, TILE), lambda s, b, *_: (s, 0)),
                pl.BlockSpec((1, 1, TILE), lambda s, b, *_: (s * tiles + b, 0, 0)),
            ],
            out_specs=[
                pl.BlockSpec((TILE, width), lambda s, b, *_: (s * tiles + b, 0)),
                pl.BlockSpec((1, 8, 2 * TILE), lambda s, b, *_: (s * tiles + b, 0, 0)),
            ],
        ),
        out_shape=[
            jax.ShapeDtypeStruct((rows, width), BF),
            jax.ShapeDtypeStruct((sequences * tiles, 8, 2 * TILE), F32),
        ],
        compiler_params=pltpu.CompilerParams(vmem_limit_bytes=VMEM_LIMIT),
        cost_estimate=pl.CostEstimate(flops=8 * 10**9, bytes_accessed=16 * 10**6, transcendentals=0),
        name="attend_forward",
    )(low, count, projected, projected, projected, key_ids, query_ids)


def attend_backward(projected, d_attended, attended, lse, windows, sequences, groups=2):
    low, count, key_ids, query_ids = windows
    rows = projected.shape[0]
    width = projected.shape[1] // 3
    length = rows // sequences
    tiles = length // TILE
    part = width // groups
    pairs = part // PAIR
    query_spec = pl.BlockSpec((TILE, part), lambda s, g, b, *_: (s * tiles + b, g))
    return pl.pallas_call(
        functools.partial(attend_backward_kernel, pairs, tiles),
        grid_spec=pltpu.PrefetchScalarGridSpec(
            num_scalar_prefetch=2,
            grid=(sequences, groups, tiles),
            in_specs=[
                query_spec,
                pl.BlockSpec((length, part), lambda s, g, b, *_: (s, groups + g)),
                pl.BlockSpec((length, part), lambda s, g, b, *_: (s, 2 * groups + g)),
                query_spec,
                query_spec,
                pl.BlockSpec((1, 8, 2 * TILE), lambda s, g, b, *_: (s * tiles + b, 0, 0)),
                pl.BlockSpec((length, TILE), lambda s, g, b, *_: (s, 0)),
                pl.BlockSpec((1, 1, TILE), lambda s, g, b, *_: (s * tiles + b, 0, 0)),
            ],
            out_specs=[
                query_spec,
                pl.BlockSpec((length, part), lambda s, g, b, *_: (s, g)),
                pl.BlockSpec((length, part), lambda s, g, b, *_: (s, g)),
            ],
            scratch_shapes=[pltpu.VMEM((length, part), F32), pltpu.VMEM((length, part), F32)],
        ),
        out_shape=[jax.ShapeDtypeStruct((rows, width), BF)] * 3,
        compiler_params=pltpu.CompilerParams(vmem_limit_bytes=VMEM_LIMIT),
        cost_estimate=pl.CostEstimate(flops=30 * 10**9, bytes_accessed=30 * 10**6, transcendentals=0),
        name="attend_backward",
    )(low, count, projected, projected, projected, d_attended, attended, lse, key_ids, query_ids)


def layer_norm(values, gain_vec, shift_vec):
    center = values - jnp.mean(values, axis=-1, keepdims=True)
    spread = jnp.mean(center * center, axis=-1, keepdims=True)
    rstd_rows = lax.rsqrt(spread + epsilon)
    scaled = center * rstd_rows
    return (scaled * gain_vec + shift_vec, scaled, rstd_rows)


def norm_backward(grad, scaled, rstd_rows, gain_vec):
    inner = grad * gain_vec
    d_input = rstd_rows * (
        inner
        - jnp.mean(inner, axis=-1, keepdims=True)
        - scaled * jnp.mean(inner * scaled, axis=-1, keepdims=True)
    )
    return (d_input, jnp.sum(grad * scaled, axis=0), jnp.sum(grad, axis=0))


def gelu_slope(values):
    return 0.5 * (1.0 + lax.erf(values * (1.0 / math.sqrt(2.0)))) + values * jnp.exp(
        -0.5 * values * values
    ) * (1.0 / math.sqrt(2.0 * math.pi))


def local(
    tokens,
    segment_ids,
    cotangent,
    w_qkv,
    b_query,
    b_value,
    w_out,
    b_out,
    gain_one,
    shift_one,
    w_in,
    b_in,
    w_ffo,
    b_ffo,
    gain_two,
    shift_two,
):
    micro, sequences, length, width = tokens.shape
    total = micro * sequences
    rows = total * length
    x = tokens.reshape(rows, width)
    seg = segment_ids.reshape(total, length)
    cot = cotangent.reshape(rows, width).astype(F32)

    def gather(a):
        return lax.all_gather(a, "shard", axis=0, tiled=True)

    full_qkv = gather(w_qkv)
    full_out = gather(w_out)
    full_in = gather(w_in)
    full_ffo = gather(w_ffo)
    small_shards = (b_query, b_value, b_out, gain_one, shift_one, b_ffo, gain_two, shift_two, b_in)
    part = b_query.shape[0]
    small = jnp.concatenate(small_shards).reshape(1, -1)
    small_full = gather(small).astype(F32)
    piece = [small_full[:, i * part : (i + 1) * part].reshape(-1) for i in range(8)]
    bq, bv, bo, g1, s1, bf, g2, s2 = piece
    bi = small_full[:, 8 * part :].reshape(-1)

    windows = windows_of(seg)
    bias_all = jnp.concatenate([bq, jnp.zeros_like(bq), bv])
    projected = (dot_nn(x, full_qkv) + bias_all).astype(BF)
    attended, lse = attend_forward(projected, windows, total)
    branch = dot_nn(attended, full_out) + bo
    normed_one, n_one, rstd_one = layer_norm(x.astype(F32) + branch, g1, s1)
    normed = normed_one.astype(BF)
    pre = dot_nn(normed, full_in) + bi
    hidden = jax.nn.gelu(pre, approximate=False).astype(BF)
    second = dot_nn(hidden, full_ffo) + bf
    output, n_two, rstd_two = layer_norm(normed.astype(F32) + second, g2, s2)
    output = output.astype(BF)

    d_res_two, d_gain_two, d_shift_two = norm_backward(cot, n_two, rstd_two, g2)
    d_second = d_res_two.astype(BF)
    d_ffo_bias = jnp.sum(d_second.astype(F32), axis=0)
    d_ffo = dot_tn(hidden, d_second)
    d_pre = (dot_nt(d_second, full_ffo) * gelu_slope(pre)).astype(BF)
    d_in_bias = jnp.sum(d_pre.astype(F32), axis=0)
    d_in = dot_tn(normed, d_pre)
    d_norm_one = d_res_two + dot_nt(d_pre, full_in)
    d_res_one, d_gain_one, d_shift_one = norm_backward(d_norm_one, n_one, rstd_one, g1)
    d_branch = d_res_one.astype(BF)
    d_out_bias = jnp.sum(d_branch.astype(F32), axis=0)
    d_out = dot_tn(attended, d_branch)
    d_attended = dot_nt(d_branch, full_out).astype(BF)
    dq, dk, dv = attend_backward(projected, d_attended, attended, lse, windows, total)
    d_projected = jnp.concatenate([dq, dk, dv], axis=1)
    d_query_bias = jnp.sum(dq.astype(F32), axis=0)
    d_value_bias = jnp.sum(dv.astype(F32), axis=0)
    d_qkv = dot_tn(x, d_projected)
    d_tokens = (d_res_one + dot_nt(d_projected, full_qkv)).astype(BF)

    def reduce(grad):
        owned = lax.psum_scatter(grad.astype(BF), "shard", scatter_dimension=0, tiled=True)
        return lax.psum(owned, "rep").astype(F32)

    smalls = (
        d_query_bias, d_value_bias, d_out_bias, d_gain_one, d_shift_one, d_ffo_bias, d_gain_two, d_shift_two,
        d_in_bias,
    )
    group = lax.axis_size("shard")
    packed = jnp.concatenate([s.reshape(group, -1) for s in smalls], axis=1)
    packed = lax.psum(packed, ("shard", "rep"))
    mine = lax.dynamic_index_in_dim(packed, lax.axis_index("shard"), 0, keepdims=False)
    sm = [mine[i * part : (i + 1) * part] for i in range(8)]
    gqb, gvb, gob, gg1, gs1, gfb, gg2, gs2 = sm
    gib = mine[8 * part :]
    return (
        output.reshape(tokens.shape),
        d_tokens.reshape(tokens.shape),
        reduce(d_qkv),
        gqb,
        gvb,
        reduce(d_out),
        gob,
        gg1,
        gs1,
        reduce(d_in),
        gib,
        reduce(d_ffo),
        gfb,
        gg2,
        gs2,
    )


def solution(mesh):
    data = P(None, ("shard", "rep"), None, None)
    matrix = P("shard", None)
    vector = P("shard")
    return jax.shard_map(
        local,
        mesh=mesh,
        in_specs=(
            data,
            P(None, ("shard", "rep"), None),
            data,
            matrix,
            vector,
            vector,
            matrix,
            vector,
            vector,
            vector,
            matrix,
            vector,
            matrix,
            vector,
            vector,
            vector,
        ),
        out_specs=(
            data,
            data,
            matrix,
            vector,
            vector,
            matrix,
            vector,
            vector,
            vector,
            matrix,
            vector,
            matrix,
            vector,
            vector,
            vector,
        ),
        check_vma=False,
    )
```

time: 1280 us -> 733 us (0.57)
  matrix products: 560 us -> 227 us
  local copies, waits for them, and re-layouts: 243 us -> 34.9 us
  other arithmetic: 178 us -> 28.3 us
  Pallas kernels: 0 us -> 128 us
  waiting for transfers between devices: 213 us -> 243 us
    dot_general x52 -> x12, matrix products: 560 us -> 227 us  [the longest x4 116 us: dot_nn(): lax.dot_general(a, b, (((1,), (0,)), ((), ())), preferred_element_type=F32)]
    pallas_call x0 -> x2, Pallas kernels: none -> 128 us  [the longest x1 85.8 us: attend_backward(): pl.pallas_call(functools.partial(attend_backward_kernel, pairs, tiles), g...]
    dynamic_update_slice x8 -> x0, local copies, waits for them, and re-layouts: 119 us -> none  [attend_backward(): lax.scan(one_block, (zeros_start, zeros_start), (query_blocks, segment_bl...]
    convert_element_type x33 -> x3, other arithmetic: 100 us -> 6.75 us  [reduce(): return lax.psum(owned, 'rep').astype(F32)]
    reduce_sum x9 -> x5, other arithmetic: 63.1 us -> 12.3 us  [the longest x1 4.69 us: local(): d_out_bias = jnp.sum(d_branch.astype(F32), axis=0)]
    unnamed x305 -> x59, local copies, waits for them, and re-layouts: 49.5 us -> 22.4 us
    while x44 -> x0, local copies, waits for them, and re-layouts: 24.5 us -> none
    unnamed x2 -> x0, blocking collectives: 23.8 us -> none
  transfers between devices with their start and end apart: 9 -> 9, of which waited for: 4 -> 6; matrix products, arithmetic and copies ran while one was open for 29% -> 25% of each run, Pallas kernels for 0% -> 6%
where the time goes in v1:
time: 733 us; the launch traced here: 726 us
  waiting for transfers between devices  243 us (33%)
  matrix products  227 us (31%)
  Pallas kernels  128 us (17%)
  blocking collectives  49.9 us (7%)
  local copies, waits for them, and re-layouts  34.9 us (5%)
  other arithmetic  28.3 us (4%)
  between operations  14.4 us (2%)
    reduce_scatter x3, waiting for transfers between devices, reduce(): lax.psum_scatter(grad.astype(BF), 'shard', scatter_dimension=0, tiled=True)  127 us
    dot_general x4, matrix products, dot_nn(): lax.dot_general(a, b, (((1,), (0,)), ((), ())), preferred_element_type=F32)  116 us
    psum x1, waiting for transfers between devices, reduce(): return lax.psum(owned, 'rep').astype(F32)  90.7 us
    pallas_call x1, Pallas kernels, attend_backward(): pl.pallas_call(functools.partial(attend_backward_kernel, pairs, tiles), g...  85.8 us
    dot_general x4, matrix products, dot_nt(): lax.dot_general(a, b, (((1,), (1,)), ((), ())), preferred_element_type=F32)  59.5 us
    dot_general x4, matrix products, dot_tn(): lax.dot_general(a, b, (((0,), (0,)), ((), ())), preferred_element_type=F32)  51.3 us
    psum x1, blocking collectives, local(): packed = lax.psum(packed, ('shard', 'rep'))  43.7 us
    pallas_call x1, Pallas kernels, attend_forward(): pl.pallas_call(functools.partial(attend_forward_kernel, pairs, tiles), gr...  42.5 us
  transfers between devices with their start and end apart: 9, of which 6 were waited for; matrix products, arithmetic and copies ran while one was open for 25% of the time, Pallas kernels for 6%

profile of v1, /device:TPU:0, one launch (start us, length us, event | category | flops | bytes accessed | tf_op | source)
XLA Modules:
  0.0 726.0 jit_solution(2545653015435964441)
XLA Ops:
  10.0 6.1 concatenate.12
  16.1 6.2 all-gather.1
  31.4 11.6 %all-gather.7.cloned.1.call-done = bf16[768,2304]{1,0:T(8,128)(2,1)} async-done(((bf16[192,2304]{1,0:T(8,128)(2,1)}), bf16[768,2304]{1,0:T(8,128)(2,1)}) %all-gather.7.cloned.1.call-update) | async-done | bytes 3538960 | tf_op jit(solution)/shard_map/all_gather | solution.py:303
  43.1 12.3 %add_convert_fusion.q_ref.k_ref.v_ref = bf16[2048,2304]{1,0:T(8,128)(2,1)} fusion(bf16[2048,768]{1,0:T(8,128)(2,1)} %bitcast.92, bf16[768,2304]{1,0:T(8,128)(2,1)} %all-gather.7.cloned.1.call-done, f32[2304]{0:T(1024)S(1)} %pad_maximum_fusion), kind=kOutput, calls=%fused_computation.27 | convolution fusion | flops 7257194496 | bytes 16131072 | tf_op jit(solution)/shard_map/dot_general | solution.py:24
  56.7 42.5 %attend_forward.1 = (bf16[2048,768]{1,0:T(8,128)(2,1)}, f32[16,8,256]{2,1,0:T(8,128)}) custom-call(s32[16]{0:T(128)} %get-tuple-element.89.low_ref, s32[16]{0:T(128)} %get-tuple-element.88.count_ref, bf16[2048,2304]{1,0:T(8,128)(2,1)} %add_convert_fusion.q_ref.k_ref.v_ref, bf16[2048,2304]{1,0:T(8,128)(2,1)} %add_convert_fusion.q_ref.k_ref.v_ref, ...), custom_call_target="tpu_custom_call" | custom-call | flops 8000000000 | bytes 16000000 | tf_op jit(solution)/shard_map/attend_forward/pallas_call | solution.py:188
  99.2 6.4 fusion.33
  109.1 81.5 %fusion.2 = (bf16[2048,3072]{1,0:T(8,128)(2,1)}, f32[2048,3072]{1,0:T(8,128)}) fusion(f32[3072]{0:T(1024)S(1)} %add.136, bf16[768,3072]{1,0:T(8,128)(2,1)} %all-gather.11.cloned.1.call-done, f32[2048,768]{1,0:T(8,128)} %copy-done.1, f32[768]{0:T(1024)S(1)} %add.133, f32[768]{0:T(1024)S(1)} %mul.138, f32[2048]{0:T(1024)S(1)} %add_rsqrt_fusion.1, ...), kind=kOutput, calls=%fused_computation.4 | convolution fusion | flops 10086776832 | bytes 48793600 | tf_op jit(solution)/shard_map/dot_general | solution.py:24
  190.6 15.8 %fusion.34 = (f32[2048]{0:T(1024)S(1)}, f32[2048,768]{1,0:T(8,128)S(1)}) fusion(f32[768]{0:T(1024)S(1)} %copy-done.17, bf16[2048,3072]{1,0:T(8,128)(2,1)} %get-tuple-element.111, bf16[3072,768]{1,0:T(8,128)(2,1)} %all-gather.13.cloned.1.call-done, f32[768]{0:T(1024)S(1)} %add.133, f32[768]{0:T(1024)S(1)} %mul.138, f32[2048]{0:T(1024)S(1)} %add_rsqrt_fusion.1, ...), kind=kOutput, calls=%fused_computation.100 | convolution fusion | flops 9677830144 | bytes 29918208 | tf_op jit(solution)/shard_map/dot_general | solution.py:24
  216.0 23.6 %convert_reduce_fusion = (f32[3072]{0:T(1024)S(1)}, bf16[2048,3072]{1,0:T(8,128)(2,1)}) fusion(f32[2048,3072]{1,0:T(8,128)} %get-tuple-element.112, f32[3072]{0:T(1024)S(1)} %add.136, bf16[3072,768]{1,0:T(8,128)(2,1)S(1)} %bitcast.91, f32[2048,768]{1,0:T(8,128)S(1)} %get-tuple-element.85), kind=kOutput, calls=%fused_computation.11 | convolution fusion | flops 9747035136 | bytes 48783360 | tf_op jit(solution)/shard_map/dot_general | solution.py:28
  239.6 18.6 %multiply_reduce_fusion = (f32[768]{0:T(1024)S(1)}, f32[2048]{0:T(1024)S(1)}, f32[2048]{0:T(1024)S(1)}, f32[768]{0:T(1024)S(1)}, f32[2048,768]{1,0:T(8,128)}) fusion(f32[2048,768]{1,0:T(8,128)S(1)} %bitcast.70, f32[2048]{0:T(1024)S(1)} %add_rsqrt_fusion.1, f32[2048]{0:T(1024)S(1)} %broadcast_multiply_fusion.4, f32[768]{0:T(1024)S(1)} %mul.138, ...), kind=kOutput, calls=%fused_computation.40 | convolution fusion | flops 9679398912 | bytes 36217856 | tf_op jit(solution)/shard_map/dot_general | solution.py:28
  258.2 4.7 convert_reduce_fusion.3
  266.9 85.8 %attend_backward.1 = (bf16[2048,768]{1,0:T(8,128)(2,1)}, bf16[2048,768]{1,0:T(8,128)(2,1)}, bf16[2048,768]{1,0:T(8,128)(2,1)}) custom-call(s32[16]{0:T(128)} %get-tuple-element.89.low_ref, s32[16]{0:T(128)} %get-tuple-element.88.count_ref, bf16[2048,2304]{1,0:T(8,128)(2,1)} %add_convert_fusion.q_ref.k_ref.v_ref, ...), custom_call_target="tpu_custom_call" | custom-call | flops 30000001024 | bytes 30000000 | tf_op jit(solution)/shard_map/attend_backward/pallas_call | solution.py:224
  360.3 9.3 %fusion.23 = bf16[768,2304]{0,1:T(8,128)(2,1)} fusion(bf16[2048,2304]{1,0:T(8,128)(2,1)S(1)} %constant_dynamic-update-slice_fusion, bf16[2048,768]{1,0:T(8,128)(2,1)S(1)} %bitcast.94), kind=kOutput, calls=%fused_computation.59 | convolution fusion | flops 7249526784 | bytes 16121856 | tf_op jit(solution)/shard_map/dot_general | solution.py:32
  369.6 5.8 copy.46
  375.4 7.4 %convolution_convert_fusion.4 = bf16[768,768]{1,0:T(8,128)(2,1)} fusion(bf16[2048,768]{1,0:T(8,128)(2,1)} %get-tuple-element.20.o_ref, f32[2048,768]{1,0:T(8,128)} %copy-done.3), kind=kOutput, calls=%fused_computation.62 | convolution fusion | flops 2418081792 | bytes 10616832 | tf_op jit(solution)/shard_map/dot_general | solution.py:32
  382.9 18.3 %convolution_convert_fusion.1 = bf16[768,3072]{1,0:T(8,128)(2,1)} fusion(bf16[2048,3072]{1,0:T(8,128)(2,1)} %get-tuple-element.117, f32[2048,768]{1,0:T(8,128)} %copy-done.1, f32[768]{0:T(1024)S(1)} %add.133, f32[768]{0:T(1024)S(1)} %mul.138, f32[2048]{0:T(1024)S(1)} %add_rsqrt_fusion.1, f32[2048]{0:T(1024)S(1)} %broadcast_multiply_fusion.4), kind=kOutput, calls=%fused_computation.57 | convolution fusion | flops 9673900032 | bytes 23615488 | tf_op jit(solution)/shard_map/dot_general | solution.py:32
  401.3 16.3 %convolution_convert_fusion = bf16[3072,768]{1,0:T(8,128)(2,1)} fusion(bf16[2048,3072]{1,0:T(8,128)(2,1)} %get-tuple-element.111, f32[2048,768]{1,0:T(8,128)} %copy-done.4), kind=kOutput, calls=%fused_computation.56 | convolution fusion | flops 9667608576 | bytes 23592960 | tf_op jit(solution)/shard_map/dot_general | solution.py:32
  417.8 11.0 %reduce-scatter.13.cloned.1.call-done = bf16[192,2304]{1,0:T(8,128)(2,1)} async-done(((bf16[768,2304]{1,0:T(8,128)(2,1)}), bf16[192,2304]{1,0:T(8,128)(2,1)}) %reduce-scatter.13.cloned.1.call-update) | async-done | bytes 884752
  431.3 26.1 %reduce-scatter.7.cloned.1.call-done = bf16[192,768]{1,0:T(8,128)(2,1)} async-done(((bf16[768,768]{1,0:T(8,128)(2,1)}), bf16[192,768]{1,0:T(8,128)(2,1)}) %reduce-scatter.7.cloned.1.call-update) | async-done | bytes 294928 | tf_op jit(solution)/shard_map/reduce_scatter | solution.py:351
  457.4 50.5 %reduce-scatter.9.cloned.1.call-done = bf16[192,3072]{1,0:T(8,128)(2,1)} async-done(((bf16[768,3072]{1,0:T(8,128)(2,1)}), bf16[192,3072]{1,0:T(8,128)(2,1)}) %reduce-scatter.9.cloned.1.call-update) | async-done | bytes 1179664 | tf_op jit(solution)/shard_map/reduce_scatter | solution.py:351
  507.9 50.5 %reduce-scatter.11.cloned.1.call-done = bf16[768,768]{1,0:T(8,128)(2,1)} async-done(((bf16[3072,768]{1,0:T(8,128)(2,1)}), bf16[768,768]{1,0:T(8,128)(2,1)}) %reduce-scatter.11.cloned.1.call-update) | async-done | bytes 1179664 | tf_op jit(solution)/shard_map/reduce_scatter | solution.py:351
  562.1 43.7 %psum.36 = f32[4,2304]{1,0:T(4,128)S(1)} all-reduce(f32[4,2304]{1,0:T(4,128)S(1)} %concatenate.15), channel_id=1, replica_groups=mesh['shard'=4,'rep'=8] {'shard','rep'}, use_global_device_ids=true, to_apply=%region_21.22 | all-reduce | flops 9216 | bytes 73728 | tf_op jit(solution)/shard_map/psum | solution.py:360
  607.1 13.3 %add_convert_fusion.1 = bf16[2048,768]{1,0:T(8,128)(2,1)} fusion(f32[2048,768]{1,0:T(8,128)} %copy-done.3, bf16[2048,2304]{1,0:T(8,128)(2,1)} %copy-done.7, bf16[768,2304]{1,0:T(8,128)(2,1)} %all-gather.7.cloned.1.call-done), kind=kOutput, calls=%fused_computation.44 | convolution fusion | flops 7250903040 | bytes 22413312 | tf_op jit(solution)/shard_map/dot_general | solution.py:28
  620.4 90.7 %all-reduce.3.cloned.1.call-done = (bf16[192,2304]{0,1:T(8,128)(2,1)}, bf16[192,768]{1,0:T(8,128)(2,1)}, bf16[192,3072]{1,0:T(8,128)(2,1)}, bf16[768,768]{1,0:T(8,128)(2,1)}) async-done(((bf16[192,2304]{0,1:T(8,128)(2,1)}, bf16[192,768]{1,0:T(8,128)(2,1)}, bf16[192,3072]{1,0:T(8,128)(2,1)}, bf16[768,768]{1,0:T(8,128)(2,1)}), (bf16[192,2304]{0,1:T(8,128)(2,1)}, bf16[192,768]{1,0:T(8,128)(2,1)}, ...) | async-done | bytes 3538960 | tf_op jit(solution)/shard_map/psum | solution.py:352
  (132 shorter events, 53.8 us)
Async XLA Ops:
  7.2 35.9 %all-gather.7.cloned.1.call-start = ((), (), s32[]{:S(2)}) async-start(), calls=%async_computation.4 | async-start | bytes 4423680 | tf_op jit(solution)/shard_map/all_gather | solution.py:303
  7.9 91.2 %all-gather.9.cloned.1.call-start = ((), (), s32[]{:S(2)}) async-start(), calls=%async_computation.5 | async-start | bytes 1474560 | tf_op jit(solution)/shard_map/all_gather | solution.py:303
  8.7 100.4 %all-gather.11.cloned.1.call-start = ((), (), s32[]{:S(2)}) async-start(), calls=%async_computation.6 | async-start | bytes 5898240 | tf_op jit(solution)/shard_map/all_gather | solution.py:303
  9.4 181.2 %all-gather.13.cloned.1.call-start = ((), (), s32[]{:S(2)}) async-start(), calls=%async_computation.7 | async-start | bytes 5898240 | tf_op jit(solution)/shard_map/all_gather | solution.py:303
  10.0 418.8 %reduce-scatter.13.cloned.1.call-start = ((), (), s32[]{:S(2)}) async-start(), calls=%async_computation.11 | async-start | bytes 4423680
  25.7 29.7 %copy-start.10 = (f32[768]{0:T(1024)}, f32[768]{0:T(1024)S(1)}, u32[]{:S(2)}) copy-start(f32[768]{0:T(1024)S(1)} %mul.147) | copy-start | bytes 9220
  43.0 12.3 %copy-start.9 = (s32[2,1,1024]{2,1,0:T(1,128)S(1)}, s32[2,1,1024]{2,1,0:T(1,128)}, u32[]{:S(2)}) copy-start(s32[2,1,1024]{2,1,0:T(1,128)} %param.17) | copy-start | bytes 24580
  109.1 81.5 %copy-start.17 = (f32[768]{0:T(1024)S(1)}, f32[768]{0:T(1024)}, u32[]{:S(2)}) copy-start(f32[768]{0:T(1024)} %add.139) | copy-start | bytes 9220
  208.4 7.6 %slice-start.2 = ((s8[4718592]{0:T(1024)(128)(4,1)}), s8[4194304]{0:T(1024)(128)(4,1)S(1)}, s32[]{:S(2)}) async-start(s8[4718592]{0:T(1024)(128)(4,1)} %bitcast.90), calls=%async_computation.15 | async-start | bytes 8388608
  211.5 4.5 slice-start.3
  211.5 28.1 %slice-start = ((s8[6291456]{0:T(1024)(128)(4,1)}), s8[4194304]{0:T(1024)(128)(4,1)S(1)}, s32[]{:S(2)}) async-start(s8[6291456]{0:T(1024)(128)(4,1)} %bitcast.69), calls=%async_computation.13 | async-start | bytes 8388608
  216.0 23.6 %copy-start.4 = (f32[2048,768]{1,0:T(8,128)}, f32[2048,768]{1,0:T(8,128)S(1)}, u32[]{:S(2)}) copy-start(f32[2048,768]{1,0:T(8,128)S(1)} %get-tuple-element.85) | copy-start | bytes 18874372
  216.0 23.6 %slice-start.1 = ((s8[6291456]{0:T(1024)(128)(4,1)}), s8[2097152]{0:T(1024)(128)(4,1)S(1)}, s32[]{:S(2)}) async-start(s8[6291456]{0:T(1024)(128)(4,1)} %bitcast.69), calls=%async_computation.14 | async-start | bytes 4194304
  258.2 4.7 copy-start.19
  355.5 4.8 copy-start.18
  375.4 82.0 %reduce-scatter.7.cloned.1.call-start = ((), (), s32[]{:S(2)}) async-start(), calls=%async_computation.8 | async-start | bytes 1474560 | tf_op jit(solution)/shard_map/reduce_scatter | solution.py:351
  382.9 125.0 %reduce-scatter.9.cloned.1.call-start = ((), (), s32[]{:S(2)}) async-start(), calls=%async_computation.9 | async-start | bytes 5898240 | tf_op jit(solution)/shard_map/reduce_scatter | solution.py:351
  401.3 157.2 %reduce-scatter.11.cloned.1.call-start = ((), (), s32[]{:S(2)}) async-start(), calls=%async_computation.10 | async-start | bytes 5898240 | tf_op jit(solution)/shard_map/reduce_scatter | solution.py:351
  417.7 140.8 %copy-start.13 = (f32[768]{0:T(1024)S(1)}, f32[768]{0:T(1024)}, u32[]{:S(2)}) copy-start(f32[768]{0:T(1024)} %get-tuple-element.76) | copy-start | bytes 9220
  417.7 144.2 %copy-start.15 = (f32[768]{0:T(1024)S(1)}, f32[768]{0:T(1024)}, u32[]{:S(2)}) copy-start(f32[768]{0:T(1024)} %get-tuple-element.84) | copy-start | bytes 9220
  417.7 144.2 %copy-start.14 = (f32[768]{0:T(1024)S(1)}, f32[768]{0:T(1024)}, u32[]{:S(2)}) copy-start(f32[768]{0:T(1024)} %get-tuple-element.72) | copy-start | bytes 9220
  417.7 293.3 %all-reduce.3.cloned.1.call-start = ((), (), s32[]{:S(2)}) async-start(), calls=%async_computation.12 | async-start | bytes 7667712 | tf_op jit(solution)/shard_map/psum | solution.py:352
  711.0 5.9 copy-start.6
  711.0 7.4 %copy-start.8 = (bf16[192,768]{1,0:T(8,128)(2,1)S(1)}, bf16[192,768]{1,0:T(8,128)(2,1)}, u32[]{:S(2)}) copy-start(bf16[192,768]{1,0:T(8,128)(2,1)} %get-tuple-element.81) | copy-start | bytes 884740
  (9 other events, 28.9 us)
Sparse Core Ops, SparseCore 0:
  9.6 33.4 all-gather.6
  44.6 17.5 all-gather.8
  63.7 37.4 all-gather.10
  102.6 37.4 all-gather.12
  375.5 53.2 reduce-scatter.12
  431.8 25.5 reduce-scatter.6
  459.9 47.9 reduce-scatter.8
  510.4 47.9 reduce-scatter.10
  563.0 147.9 all-reduce.2

commit v2 on v1

--- a/solution.py
+++ b/solution.py
@@ -250,28 +250,336 @@
     )(low, count, projected, projected, projected, d_attended, attended, lse, key_ids, query_ids)
 
 
-def layer_norm(values, gain_vec, shift_vec):
-    center = values - jnp.mean(values, axis=-1, keepdims=True)
-    spread = jnp.mean(center * center, axis=-1, keepdims=True)
-    rstd_rows = lax.rsqrt(spread + epsilon)
-    scaled = center * rstd_rows
-    return (scaled * gain_vec + shift_vec, scaled, rstd_rows)
-
-
-def norm_backward(grad, scaled, rstd_rows, gain_vec):
-    inner = grad * gain_vec
-    d_input = rstd_rows * (
-        inner
-        - jnp.mean(inner, axis=-1, keepdims=True)
-        - scaled * jnp.mean(inner * scaled, axis=-1, keepdims=True)
-    )
-    return (d_input, jnp.sum(grad * scaled, axis=0), jnp.sum(grad, axis=0))
-
-
-def gelu_slope(values):
-    return 0.5 * (1.0 + lax.erf(values * (1.0 / math.sqrt(2.0)))) + values * jnp.exp(
-        -0.5 * values * values
-    ) * (1.0 / math.sqrt(2.0 * math.pi))
+def row_mean(values):
+    return jnp.mean(values, axis=-1, keepdims=True)
+
+
+def fold_rows(values):
+    rows, width = values.shape
+    return jnp.sum(values.reshape(rows // 8, 8, width), axis=0)
+
+
+def load_pieces(starts_ref, pieces, targets, sems):
+    copies = []
+    for n, (piece, target) in enumerate(zip(pieces, targets)):
+        height = piece.shape[0]
+        start = pl.multiple_of(starts_ref[n], math.gcd(height, 128))
+        copies.append(pltpu.make_async_copy(piece, target.at[pl.ds(start, height)], sems.at[n]))
+    for copy in copies:
+        copy.start()
+    for copy in copies:
+        copy.wait()
+
+
+def gelu_parts(values):
+    bell = jnp.exp(values * values * -0.5)
+    t = 1.0 / (1.0 + jnp.abs(values) * (0.3275911 / math.sqrt(2.0)))
+    poly = t * (
+        0.5 * 0.254829592
+        + t * (0.5 * -0.284496736 + t * (0.5 * 1.421413741 + t * (0.5 * -1.453152027 + t * (0.5 * 1.061405429))))
+    )
+    tail = poly * bell
+    phi = jnp.where(values >= 0.0, 1.0 - tail, tail)
+    return values * phi, phi + values * bell * (1.0 / math.sqrt(2.0 * math.pi))
+
+
+def project_kernel(count, starts_ref, x_ref, bias_ref, *refs):
+    pieces = refs[:count]
+    o_ref, weight, sems = refs[count:]
+
+    @pl.when(pl.program_id(0) == 0)
+    def _():
+        load_pieces(starts_ref, pieces, [weight] * count, sems)
+
+    o_ref[...] = (dot_nn(x_ref[...], weight[...]) + bias_ref[...]).astype(BF)
+
+
+FFN_CHUNK = 512
+
+
+def layer_forward_kernel(
+    counts, starts_ref, x_ref, att_ref, cot_ref, vec_ref, bin_ref, *refs
+):
+    total = sum(counts)
+    pieces = refs[:total]
+    (
+        out_ref, normed_ref, none_ref, rstd_ref, dsec_ref, hidden_ref, slope_ref, sums_ref,
+        w_out, w_in, w_ffo, sems,
+    ) = refs[total:]
+    targets = [w_out] * counts[0] + [w_in] * counts[1] + [w_ffo] * counts[2]
+
+    @pl.when(pl.program_id(0) == 0)
+    def _():
+        load_pieces(starts_ref, pieces, targets, sems)
+        sums_ref[...] = jnp.zeros_like(sums_ref)
+
+    b_out, gain_one, shift_one, b_ffo, gain_two, shift_two = [vec_ref[i : i + 1, :] for i in range(6)]
+    res = x_ref[...].astype(F32) + (dot_nn(att_ref[...], w_out[...]) + b_out)
+    center = res - row_mean(res)
+    rstd = lax.rsqrt(row_mean(center * center) + epsilon)
+    n_one = center * rstd
+    normed = (n_one * gain_one + shift_one).astype(BF)
+    normed_ref[...] = normed
+    none_ref[...] = n_one.astype(BF)
+    rstd_ref[...] = jnp.broadcast_to(rstd, rstd_ref.shape)
+    hidden_width = w_in.shape[1]
+    second = None
+    pres = []
+    for c in range(0, hidden_width, FFN_CHUNK):
+        cols = slice(c, c + FFN_CHUNK)
+        pre = dot_nn(normed, w_in[:, cols]) + bin_ref[:, cols]
+        value, slope = gelu_parts(pre)
+        value = value.astype(BF)
+        hidden_ref[:, cols] = value
+        slope_ref[:, cols] = slope.astype(BF)
+        term = dot_nn(value, w_ffo[cols, :])
+        second = term if second is None else second + term
+    res = normed.astype(F32) + (second + b_ffo)
+    center = res - row_mean(res)
+    rstd = lax.rsqrt(row_mean(center * center) + epsilon)
+    n_two = center * rstd
+    out_ref[...] = (n_two * gain_two + shift_two).astype(BF)
+    cot = cot_ref[...].astype(F32)
+    inner = cot * gain_two
+    d_second = (rstd * (inner - row_mean(inner) - n_two * row_mean(inner * n_two))).astype(BF)
+    dsec_ref[...] = d_second
+    sums_ref[0:8, :] += fold_rows(cot * n_two)
+    sums_ref[8:16, :] += fold_rows(cot)
+    sums_ref[16:24, :] += fold_rows(d_second.astype(F32))
+
+
+def layer_backward_kernel(counts, starts_ref, dsec_ref, slope_ref, none_ref, rstd_ref, vec_ref, *refs):
+    total = sum(counts)
+    pieces = refs[:total]
+    dpre_ref, dbranch_ref, datt_ref, sums_ref, bin_ref, w_out, w_in, w_ffo, sems = refs[total:]
+    targets = [w_out] * counts[0] + [w_in] * counts[1] + [w_ffo] * counts[2]
+
+    @pl.when(pl.program_id(0) == 0)
+    def _():
+        load_pieces(starts_ref, pieces, targets, sems)
+        sums_ref[...] = jnp.zeros_like(sums_ref)
+        bin_ref[...] = jnp.zeros_like(bin_ref)
+
+    gain_one = vec_ref[1:2, :]
+    d_second = dsec_ref[...]
+    d_norm = d_second.astype(F32)
+    for c in range(0, w_in.shape[1], FFN_CHUNK):
+        cols = slice(c, c + FFN_CHUNK)
+        d_pre = (dot_nt(d_second, w_ffo[cols, :]) * slope_ref[:, cols].astype(F32)).astype(BF)
+        dpre_ref[:, cols] = d_pre
+        bin_ref[:, cols] += fold_rows(d_pre.astype(F32))
+        d_norm = d_norm + dot_nt(d_pre, w_in[:, cols])
+    n_one = none_ref[...].astype(F32)
+    inner = d_norm * gain_one
+    d_res = rstd_ref[:, 0:1] * (inner - row_mean(inner) - n_one * row_mean(inner * n_one))
+    d_branch = d_res.astype(BF)
+    dbranch_ref[...] = d_branch
+    datt_ref[...] = dot_nt(d_branch, w_out[...]).astype(BF)
+    sums_ref[0:8, :] += fold_rows(d_norm * n_one)
+    sums_ref[8:16, :] += fold_rows(d_norm)
+    sums_ref[16:24, :] += fold_rows(d_branch.astype(F32))
+
+
+def input_grad_kernel(count, starts_ref, dbranch_ref, dq_ref, dk_ref, dv_ref, *refs):
+    pieces = refs[:count]
+    o_ref, weight, sems = refs[count:]
+
+    @pl.when(pl.program_id(0) == 0)
+    def _():
+        load_pieces(starts_ref, pieces, [weight] * count, sems)
+
+    width = dq_ref.shape[1]
+    total = dbranch_ref[...].astype(F32)
+    for n, ref in enumerate((dq_ref, dk_ref, dv_ref)):
+        total = total + dot_nt(ref[...], weight[:, n * width : (n + 1) * width])
+    o_ref[...] = total.astype(BF)
+
+
+def weight_grad_rows_kernel(owner_ref, a_ref, b_ref, keep_ref, pass_ref, send_ref):
+    step = pl.program_id(0)
+    part = dot_tn(a_ref[...], b_ref[...]).astype(BF)
+
+    @pl.when(step < 2)
+    def _():
+        send_ref[...] = part
+
+    @pl.when(step == 2)
+    def _():
+        pass_ref[...] = part
+
+    @pl.when(step == 3)
+    def _():
+        keep_ref[...] = part
+
+
+def weight_grad_cols_kernel(slots, owner_ref, a_ref, b_ref, keep_ref, pass_ref, send_ref, held):
+    part = dot_tn(a_ref[...], b_ref[...]).astype(BF)
+    height = keep_ref.shape[0]
+    for owner in range(4):
+        held[owner_ref[owner]] = part[owner * height : (owner + 1) * height]
+    keep_ref[...] = held[0]
+    pass_ref[...] = held[1]
+    send_ref[0:height, :] = held[2]
+    send_ref[height:, :] = held[3]
+
+
+PARAMS = pltpu.CompilerParams(vmem_limit_bytes=VMEM_LIMIT)
+
+
+def cost(flops, bytes_accessed):
+    return pl.CostEstimate(flops=int(flops), bytes_accessed=int(bytes_accessed), transcendentals=0)
+
+
+def whole_spec(array):
+    zeros = (0,) * array.ndim
+    return pl.BlockSpec(array.shape, lambda *_: zeros)
+
+
+ANY = pl.BlockSpec(memory_space=pl.ANY)
+
+
+def row_call(kernel, name, rows, block, scalars, blocked, fixed, pieces, outs, accs, scratch, flops):
+    in_specs = (
+        [pl.BlockSpec((block, a.shape[1]), lambda i, *_: (i, 0)) for a in blocked]
+        + [whole_spec(a) for a in fixed]
+        + [ANY] * len(pieces)
+    )
+    out_specs = [pl.BlockSpec((block, s.shape[1]), lambda i, *_: (i, 0)) for s in outs] + [
+        whole_spec(s) for s in accs
+    ]
+    moved = sum(a.size * a.dtype.itemsize for a in list(blocked) + list(pieces) + list(outs))
+    return pl.pallas_call(
+        kernel,
+        grid_spec=pltpu.PrefetchScalarGridSpec(
+            num_scalar_prefetch=1,
+            grid=(rows // block,),
+            in_specs=in_specs,
+            out_specs=out_specs,
+            scratch_shapes=list(scratch) + [pltpu.SemaphoreType.DMA((len(pieces),))],
+        ),
+        out_shape=list(outs) + list(accs),
+        compiler_params=PARAMS,
+        cost_estimate=cost(flops, moved),
+        name=name,
+    )(scalars, *blocked, *fixed, *pieces)
+
+
+def shaped(*shape, dtype=BF):
+    return jax.ShapeDtypeStruct(shape, dtype)
+
+
+def weight_grad(slots, a, b, name):
+    rows, height = a.shape
+    width = b.shape[1]
+    part = height // 4
+    flops = 2 * rows * height * width
+    moved = 2 * (rows * height + rows * width + height * width)
+    if part % 128 == 0:
+        return pl.pallas_call(
+            weight_grad_rows_kernel,
+            grid_spec=pltpu.PrefetchScalarGridSpec(
+                num_scalar_prefetch=1,
+                grid=(4,),
+                in_specs=[
+                    pl.BlockSpec((rows, part), lambda t, s: (0, s[4 + t])),
+                    pl.BlockSpec((rows, width), lambda t, s: (0, 0)),
+                ],
+                out_specs=[
+                    pl.BlockSpec((part, width), lambda t, s: (0, 0)),
+                    pl.BlockSpec((part, width), lambda t, s: (0, 0)),
+                    pl.BlockSpec((part, width), lambda t, s: (jnp.minimum(t, 1), 0)),
+                ],
+            ),
+            out_shape=[shaped(part, width), shaped(part, width), shaped(2 * part, width)],
+            compiler_params=PARAMS,
+            cost_estimate=cost(flops, moved),
+            name=name,
+        )(slots, a, b)
+    block = min(width, 768)
+    return pl.pallas_call(
+        functools.partial(weight_grad_cols_kernel, 4),
+        grid_spec=pltpu.PrefetchScalarGridSpec(
+            num_scalar_prefetch=1,
+            grid=(width // block,),
+            in_specs=[
+                pl.BlockSpec((rows, height), lambda t, s: (0, 0)),
+                pl.BlockSpec((rows, block), lambda t, s: (0, t)),
+            ],
+            out_specs=[
+                pl.BlockSpec((part, block), lambda t, s: (0, t)),
+                pl.BlockSpec((part, block), lambda t, s: (0, t)),
+                pl.BlockSpec((2 * part, block), lambda t, s: (0, t)),
+            ],
+            scratch_shapes=[pltpu.VMEM((4, part, block), BF)],
+        ),
+        out_shape=[shaped(part, width), shaped(part, width), shaped(2 * part, width)],
+        compiler_params=PARAMS,
+        cost_estimate=cost(flops, moved),
+        name=name,
+    )(slots, a, b)
+
+
+def swap(array, axis, bit):
+    size = lax.axis_size(axis)
+    return lax.ppermute(array, axis, [(i, i ^ bit) for i in range(size)])
+
+
+def gather_pieces(shard):
+    height = shard.shape[0]
+    if lax.axis_size("shard") != 4 or lax.axis_size("rep") % 2:
+        return [(lax.all_gather(shard, "shard", axis=0, tiled=True), jnp.int32(0))]
+    me = lax.axis_index("shard")
+    side = lax.rem(lax.axis_index("rep"), 2)
+    half = height // 2
+    mine = lax.dynamic_slice_in_dim(shard, side * half, half, axis=0)
+    direct = swap(mine, "shard", 2)
+    relayed = swap(direct, "rep", 1)
+    near = me * height
+    core = (me ^ 1) * height
+    far = (me ^ 2) * height
+    cross = (me ^ 3) * height
+    return [
+        (shard, near),
+        (swap(shard, "shard", 1), core),
+        (direct, far + side * half),
+        (relayed, far + (1 - side) * half),
+        (swap(direct, "shard", 1), cross + side * half),
+        (swap(relayed, "shard", 1), cross + (1 - side) * half),
+    ]
+
+
+def added(*terms):
+    return functools.reduce(jnp.add, [t.astype(F32) for t in terms]).astype(BF)
+
+
+def reduce_owned(parts):
+    keep, passed, sent = parts
+    height = keep.shape[0]
+    come = swap(sent, "shard", 1)
+    onward = swap(added(passed, come[height:]), "shard", 2)
+    owned = added(keep, come[:height], onward)
+    place = lax.axis_index("rep")
+    half, quarter = height // 2, height // 4
+    y = lax.rem(place, 2)
+    z = lax.rem(place // 2, 2)
+    away = lax.dynamic_slice_in_dim(owned, (1 - y) * half, half, axis=0)
+    stay = lax.dynamic_slice_in_dim(owned, y * half, half, axis=0)
+    stay = added(stay, swap(away, "rep", 1))
+    away = lax.dynamic_slice_in_dim(stay, (1 - z) * quarter, quarter, axis=0)
+    stay = lax.dynamic_slice_in_dim(stay, z * quarter, quarter, axis=0)
+    stay = added(stay, swap(away, "rep", 2))
+    stay = added(stay, swap(stay, "rep", 4))
+    other = swap(stay, "rep", 2)
+    pair = jnp.where(z == 0, jnp.stack([stay, other]), jnp.stack([other, stay])).reshape(half, -1)
+    other = swap(pair, "rep", 1)
+    both = jnp.where(y == 0, jnp.stack([pair, other]), jnp.stack([other, pair])).reshape(height, -1)
+    return both.astype(F32)
+
+
+def reduce_plain(a, b):
+    grad = dot_tn(a, b).astype(BF)
+    owned = lax.psum_scatter(grad, "shard", scatter_dimension=0, tiled=True)
+    return lax.psum(owned, "rep").astype(F32)
 
 
 def local(
@@ -295,86 +603,173 @@
     micro, sequences, length, width = tokens.shape
     total = micro * sequences
     rows = total * length
+    group = lax.axis_size("shard")
+    hidden_width = w_in.shape[1]
     x = tokens.reshape(rows, width)
     seg = segment_ids.reshape(total, length)
-    cot = cotangent.reshape(rows, width).astype(F32)
-
-    def gather(a):
-        return lax.all_gather(a, "shard", axis=0, tiled=True)
-
-    full_qkv = gather(w_qkv)
-    full_out = gather(w_out)
-    full_in = gather(w_in)
-    full_ffo = gather(w_ffo)
+    cot = cotangent.reshape(rows, width)
+    me = lax.axis_index("shard")
+    direct = group == 4 and lax.axis_size("rep") == 8
+
+    part = b_query.shape[0]
     small_shards = (b_query, b_value, b_out, gain_one, shift_one, b_ffo, gain_two, shift_two, b_in)
-    part = b_query.shape[0]
     small = jnp.concatenate(small_shards).reshape(1, -1)
-    small_full = gather(small).astype(F32)
-    piece = [small_full[:, i * part : (i + 1) * part].reshape(-1) for i in range(8)]
-    bq, bv, bo, g1, s1, bf, g2, s2 = piece
-    bi = small_full[:, 8 * part :].reshape(-1)
+    if direct:
+        near = swap(small, "shard", 1)
+        pair = jnp.concatenate([small, near], axis=0)
+        four = jnp.concatenate([pair, swap(pair, "shard", 2)], axis=0)
+        order = [jnp.bitwise_xor(me, o) for o in range(4)]
+        small_full = jnp.concatenate([lax.dynamic_slice_in_dim(four, o, 1, axis=0) for o in order], axis=0)
+    else:
+        small_full = lax.all_gather(small, "shard", axis=0, tiled=True)
+    small_full = small_full.astype(F32)
+    vectors = [small_full[:, i * part : (i + 1) * part].reshape(1, -1) for i in range(8)]
+    bias_all = jnp.concatenate([vectors[0], jnp.zeros_like(vectors[0]), vectors[1]], axis=1)
+    vec = jnp.concatenate(vectors[2:] + [jnp.zeros((2, width), F32)], axis=0)
+    bias_in = small_full[:, 8 * part :].reshape(1, -1)
+
+    qkv_pieces = gather_pieces(w_qkv)
+    out_pieces = gather_pieces(w_out)
+    in_pieces = gather_pieces(w_in)
+    ffo_pieces = gather_pieces(w_ffo)
+
+    def arrays(pieces):
+        return [p[0] for p in pieces]
+
+    def starts(pieces):
+        return jnp.stack([jnp.asarray(p[1], jnp.int32) for p in pieces])
 
     windows = windows_of(seg)
-    bias_all = jnp.concatenate([bq, jnp.zeros_like(bq), bv])
-    projected = (dot_nn(x, full_qkv) + bias_all).astype(BF)
+    block = 256
+    qkv_starts = starts(qkv_pieces)
+    (projected,) = row_call(
+        functools.partial(project_kernel, len(qkv_pieces)),
+        "project",
+        rows,
+        block,
+        qkv_starts,
+        [x],
+        [bias_all],
+        arrays(qkv_pieces),
+        [shaped(rows, 3 * width)],
+        [],
+        [pltpu.VMEM((width, 3 * width), BF)],
+        6 * rows * width * width,
+    )
     attended, lse = attend_forward(projected, windows, total)
-    branch = dot_nn(attended, full_out) + bo
-    normed_one, n_one, rstd_one = layer_norm(x.astype(F32) + branch, g1, s1)
-    normed = normed_one.astype(BF)
-    pre = dot_nn(normed, full_in) + bi
-    hidden = jax.nn.gelu(pre, approximate=False).astype(BF)
-    second = dot_nn(hidden, full_ffo) + bf
-    output, n_two, rstd_two = layer_norm(normed.astype(F32) + second, g2, s2)
-    output = output.astype(BF)
-
-    d_res_two, d_gain_two, d_shift_two = norm_backward(cot, n_two, rstd_two, g2)
-    d_second = d_res_two.astype(BF)
-    d_ffo_bias = jnp.sum(d_second.astype(F32), axis=0)
-    d_ffo = dot_tn(hidden, d_second)
-    d_pre = (dot_nt(d_second, full_ffo) * gelu_slope(pre)).astype(BF)
-    d_in_bias = jnp.sum(d_pre.astype(F32), axis=0)
-    d_in = dot_tn(normed, d_pre)
-    d_norm_one = d_res_two + dot_nt(d_pre, full_in)
-    d_res_one, d_gain_one, d_shift_one = norm_backward(d_norm_one, n_one, rstd_one, g1)
-    d_branch = d_res_one.astype(BF)
-    d_out_bias = jnp.sum(d_branch.astype(F32), axis=0)
-    d_out = dot_tn(attended, d_branch)
-    d_attended = dot_nt(d_branch, full_out).astype(BF)
+    layer_pieces = out_pieces + in_pieces + ffo_pieces
+    counts = (len(out_pieces), len(in_pieces), len(ffo_pieces))
+    layer_starts = starts(layer_pieces)
+    weights_scratch = [
+        pltpu.VMEM((width, width), BF),
+        pltpu.VMEM((width, hidden_width), BF),
+        pltpu.VMEM((hidden_width, width), BF),
+    ]
+    layer_flops = 2 * rows * width * (width + 2 * hidden_width)
+    output, normed, n_one, rstd_one, d_second, hidden, slope, sums_two = row_call(
+        functools.partial(layer_forward_kernel, counts),
+        "layer_forward",
+        rows,
+        block,
+        layer_starts,
+        [x, attended, cot],
+        [vec, bias_in],
+        arrays(layer_pieces),
+        [
+            shaped(rows, width),
+            shaped(rows, width),
+            shaped(rows, width),
+            shaped(rows, 128, dtype=F32),
+            shaped(rows, width),
+            shaped(rows, hidden_width),
+            shaped(rows, hidden_width),
+        ],
+        [shaped(24, width, dtype=F32)],
+        weights_scratch,
+        layer_flops,
+    )
+
+    place = [jnp.bitwise_xor(me, o) for o in range(4)]
+    slots = jnp.stack(
+        [(p % 2) * 2 + p // 2 for p in place] + [jnp.bitwise_xor(me, j) for j in (1, 3, 2, 0)]
+    ).astype(jnp.int32)
+
+    def weight_terms(a, b, name):
+        if direct:
+            return reduce_owned(weight_grad(slots, a, b, name))
+        return reduce_plain(a, b)
+
+    grad_ffo = weight_terms(hidden, d_second, "grad_ffo")
+    d_pre, d_branch, d_attended, sums_one, sums_in = row_call(
+        functools.partial(layer_backward_kernel, counts),
+        "layer_backward",
+        rows,
+        block,
+        layer_starts,
+        [d_second, slope, n_one, rstd_one],
+        [vec],
+        arrays(layer_pieces),
+        [shaped(rows, hidden_width), shaped(rows, width), shaped(rows, width)],
+        [shaped(24, width, dtype=F32), shaped(8, hidden_width, dtype=F32)],
+        weights_scratch,
+        layer_flops,
+    )
+    grad_in = weight_terms(normed, d_pre, "grad_in")
+    grad_out = weight_terms(attended, d_branch, "grad_out")
     dq, dk, dv = attend_backward(projected, d_attended, attended, lse, windows, total)
-    d_projected = jnp.concatenate([dq, dk, dv], axis=1)
+    grad_q = weight_terms(x, dq, "grad_q")
+    grad_k = weight_terms(x, dk, "grad_k")
+    grad_v = weight_terms(x, dv, "grad_v")
+    (d_tokens,) = row_call(
+        functools.partial(input_grad_kernel, len(qkv_pieces)),
+        "input_grad",
+        rows,
+        block,
+        qkv_starts,
+        [d_branch, dq, dk, dv],
+        [],
+        arrays(qkv_pieces),
+        [shaped(rows, width)],
+        [],
+        [pltpu.VMEM((width, 3 * width), BF)],
+        6 * rows * width * width,
+    )
     d_query_bias = jnp.sum(dq.astype(F32), axis=0)
     d_value_bias = jnp.sum(dv.astype(F32), axis=0)
-    d_qkv = dot_tn(x, d_projected)
-    d_tokens = (d_res_one + dot_nt(d_projected, full_qkv)).astype(BF)
-
-    def reduce(grad):
-        owned = lax.psum_scatter(grad.astype(BF), "shard", scatter_dimension=0, tiled=True)
-        return lax.psum(owned, "rep").astype(F32)
-
+
+    def folded(sums):
+        return [jnp.sum(sums[i : i + 8], axis=0) for i in range(0, sums.shape[0], 8)]
+
+    d_gain_two, d_shift_two, d_ffo_bias = folded(sums_two)
+    d_gain_one, d_shift_one, d_out_bias = folded(sums_one)
+    (d_in_bias,) = folded(sums_in)
     smalls = (
         d_query_bias, d_value_bias, d_out_bias, d_gain_one, d_shift_one, d_ffo_bias, d_gain_two, d_shift_two,
         d_in_bias,
     )
-    group = lax.axis_size("shard")
     packed = jnp.concatenate([s.reshape(group, -1) for s in smalls], axis=1)
-    packed = lax.psum(packed, ("shard", "rep"))
-    mine = lax.dynamic_index_in_dim(packed, lax.axis_index("shard"), 0, keepdims=False)
+    if direct:
+        for axis, bit in (("shard", 1), ("shard", 2), ("rep", 1), ("rep", 2), ("rep", 4)):
+            packed = packed + swap(packed, axis, bit)
+    else:
+        packed = lax.psum(packed, ("shard", "rep"))
+    mine = lax.dynamic_index_in_dim(packed, me, 0, keepdims=False)
     sm = [mine[i * part : (i + 1) * part] for i in range(8)]
     gqb, gvb, gob, gg1, gs1, gfb, gg2, gs2 = sm
     gib = mine[8 * part :]
     return (
         output.reshape(tokens.shape),
         d_tokens.reshape(tokens.shape),
-        reduce(d_qkv),
+        jnp.concatenate([grad_q, grad_k, grad_v], axis=1),
         gqb,
         gvb,
-        reduce(d_out),
+        grad_out,
         gob,
         gg1,
         gs1,
-        reduce(d_in),
+        grad_in,
         gib,
-        reduce(d_ffo),
+        grad_ffo,
         gfb,
         gg2,
         gs2,

time: 733 us -> 600 us (0.82)
  matrix products: 227 us -> 0 us
  Pallas kernels: 128 us -> 327 us
  waiting for transfers between devices: 243 us -> 156 us
  starting transfers between devices: 0.36 us -> 65.8 us
  blocking collectives: 49.9 us -> 0 us
  local copies, waits for them, and re-layouts: 34.9 us -> 18.6 us
  between operations: 14.4 us -> 2 us
  other arithmetic: 28.3 us -> 18.2 us
    dot_general x12 -> x0, matrix products: 227 us -> none  [the longest x4 116 us: dot_nn(): lax.dot_general(a, b, (((1,), (0,)), ((), ())), preferred_element_type=F32)]
    pallas_call x0 -> x10, Pallas kernels: none -> 190 us  [the longest x4 129 us: row_call(): pl.pallas_call(kernel, grid_spec=pltpu.PrefetchScalarGridSpec(num_scalar_...]
    ppermute x0 -> x69, waiting for transfers between devices: none -> 156 us  [swap(): return lax.ppermute(array, axis, [(i, i ^ bit) for i in range(size)])]
    reduce_scatter x3 -> x0, waiting for transfers between devices: 127 us -> none  [reduce(): lax.psum_scatter(grad.astype(BF), 'shard', scatter_dimension=0, tiled=True)]
    psum x1 -> x0, waiting for transfers between devices: 90.7 us -> none  [reduce(): return lax.psum(owned, 'rep').astype(F32)]
    ppermute x0 -> x69, starting transfers between devices: none -> 65.8 us  [swap(): return lax.ppermute(array, axis, [(i, i ^ bit) for i in range(size)])]
    psum x1 -> x0, blocking collectives: 43.7 us -> none  [local(): packed = lax.psum(packed, ('shard', 'rep'))]
    unnamed x59 -> x55, local copies, waits for them, and re-layouts: 22.4 us -> 2.18 us
  transfers between devices with their start and end apart: 9 -> 69, of which waited for: 6 -> 27; matrix products, arithmetic and copies ran while one was open for 25% -> 4% of each run, Pallas kernels for 6% -> 19%
where the time goes in v2:
time: 600 us; the launch traced here: 588 us
  Pallas kernels  327 us (54%)
  waiting for transfers between devices  156 us (26%)
  starting transfers between devices  65.8 us (11%)
  local copies, waits for them, and re-layouts  18.6 us (3%)
  other arithmetic  18.2 us (3%)
    ppermute x69, waiting for transfers between devices, swap(): return lax.ppermute(array, axis, [(i, i ^ bit) for i in range(size)])  156 us
    pallas_call x4, Pallas kernels, row_call(): pl.pallas_call(kernel, grid_spec=pltpu.PrefetchScalarGridSpec(num_scalar_...  129 us
    pallas_call x1, Pallas kernels, attend_backward(): pl.pallas_call(functools.partial(attend_backward_kernel, pairs, tiles), g...  92.4 us
    ppermute x69, starting transfers between devices, swap(): return lax.ppermute(array, axis, [(i, i ^ bit) for i in range(size)])  65.8 us
    pallas_call x1, Pallas kernels, attend_forward(): pl.pallas_call(functools.partial(attend_forward_kernel, pairs, tiles), gr...  44.8 us
    pallas_call x5, Pallas kernels, weight_grad(): pl.pallas_call(functools.partial(weight_grad_cols_kernel, 4), grid_spec=p...  44.7 us
    pallas_call x1, Pallas kernels, weight_grad(): pl.pallas_call(weight_grad_rows_kernel, grid_spec=pltpu.PrefetchScalarGri...  16.5 us
  transfers between devices with their start and end apart: 69, of which 27 were waited for; matrix products, arithmetic and copies ran while one was open for 4% of the time, Pallas kernels for 19%

profile of v2, /device:TPU:0, one launch (start us, length us, event | category | flops | bytes accessed | tf_op | source)
XLA Modules:
  0.0 588.0 jit_solution(16313407454834716956)
XLA Ops:
  0.7 6.2 %concatenate.28 = bf16[2304]{0:T(1024)(128)(2,1)S(1)} concatenate(bf16[192]{0:T(256)(128)(2,1)} %param.20, bf16[192]{0:T(256)(128)(2,1)} %param.21, bf16[192]{0:T(256)(128)(2,1)} %param.23, bf16[192]{0:T(256)(128)(2,1)} %param.24, bf16[192]{0:T(256)(128)(2,1)} %param.25, bf16[192]{0:T(256)(128)(2,1)} %param.29, bf16[192]{0:T(256)(128)(2,1)} %param.30, bf16[192]{0:T(256)(128)(2,1)} %param.31, ...), dimensions={0} | concatenate | bytes 9216 | tf_op jit(solution)/shard_map/concatenate | solution.py:616
  18.9 6.4 %collective-permute-done.1 = bf16[2,2304]{1,0:T(2,128)(2,1)S(1)} collective-permute-done((bf16[2,2304]{1,0:T(2,128)(2,1)S(1)}, bf16[2,2304]{1,0:T(2,128)(2,1)S(1)}, u32[]{:S(2)}, u32[]{:S(2)}) %collective-permute-start.1) | collective-permute-done | bytes 9248 | tf_op jit(solution)/shard_map/ppermute | solution.py:524
  35.5 5.2 collective-permute-done.4.refs_3_
  48.1 9.7 %collective-permute-done.18.refs_14_ = bf16[384,768]{1,0:T(8,128)(2,1)} collective-permute-done((bf16[384,768]{1,0:T(8,128)(2,1)S(1)}, bf16[384,768]{1,0:T(8,128)(2,1)}, u32[]{:S(2)}, u32[]{:S(2)}) %collective-permute-start.18) | collective-permute-done | bytes 589856 | tf_op jit(solution)/shard_map/ppermute | solution.py:524
  60.0 14.3 %project.1.q_ref.k_ref.v_ref = bf16[2048,2304]{1,0:T(8,128)(2,1)} custom-call(s32[6]{0:T(128)} %stack.238.starts_ref, bf16[2048,768]{1,0:T(8,128)(2,1)} %bitcast.140, f32[1,2304]{1,0:T(1,128)} %fusion.bias_ref, bf16[192,2304]{1,0:T(8,128)(2,1)} %refs_0_.7, bf16[192,2304]{1,0:T(8,128)(2,1)} %collective-permute-done.2.refs_1_, bf16[96,2304]{1,0:T(8,128)(2,1)} %copy-done.21, ...), custom_call_target="tpu_custom_call" | custom-call | flops 7247757312 | bytes 16121856 | tf_op jit(solution)/shard_map/project/pallas_call | solution.py:451
  75.0 11.5 %collective-permute-done.19.refs_15_ = bf16[384,768]{1,0:T(8,128)(2,1)} collective-permute-done((bf16[384,768]{1,0:T(8,128)(2,1)}, bf16[384,768]{1,0:T(8,128)(2,1)}, u32[]{:S(2)}, u32[]{:S(2)}) %collective-permute-start.19) | collective-permute-done | bytes 589856 | tf_op jit(solution)/shard_map/ppermute | solution.py:524
  87.8 44.8 %attend_forward.1 = (bf16[2048,768]{1,0:T(8,128)(2,1)}, f32[16,8,256]{2,1,0:T(8,128)}) custom-call(s32[16]{0:T(128)} %get-tuple-element.126.low_ref, s32[16]{0:T(128)} %get-tuple-element.125.count_ref, bf16[2048,2304]{1,0:T(8,128)(2,1)} %project.1.q_ref.k_ref.v_ref, bf16[2048,2304]{1,0:T(8,128)(2,1)} %project.1.q_ref.k_ref.v_ref, ...), custom_call_target="tpu_custom_call" | custom-call | flops 8000000000 | bytes 16000000 | tf_op jit(solution)/shard_map/attend_forward/pallas_call | solution.py:188
  133.6 59.4 %layer_forward.1 = (bf16[2048,768]{1,0:T(8,128)(2,1)}, bf16[2048,768]{1,0:T(8,128)(2,1)}, bf16[2048,768]{1,0:T(8,128)(2,1)}, f32[2048,128]{1,0:T(8,128)}, bf16[2...) custom-call(s32[18]{0:T(128)} %stack.237.starts_ref, ...), custom_call_target="tpu_custom_call" | custom-call | flops 21743271936 | bytes 58851328 | tf_op jit(solution)/shard_map/layer_forward/pallas_call | solution.py:451
  193.1 16.5 %grad_ffo.1 = (bf16[768,768]{1,0:T(8,128)(2,1)}, bf16[768,768]{1,0:T(8,128)(2,1)}, bf16[1536,768]{1,0:T(8,128)(2,1)}) custom-call(s32[8]{0:T(128)} %stack.247.owner_ref, bf16[2048,3072]{1,0:T(8,128)(2,1)} %get-tuple-element.83.a_ref, bf16[2048,768]{1,0:T(8,128)(2,1)} %get-tuple-element.53.dsec_ref.b_ref), custom_call_target="tpu_custom_call" | custom-call | flops 9663676416 | bytes 20447232 | tf_op jit(solution)/shard_map/grad_ffo/pallas_call | solution.py:478
  209.6 39.5 %layer_backward.1 = (bf16[2048,3072]{1,0:T(8,128)(2,1)}, bf16[2048,768]{1,0:T(8,128)(2,1)}, bf16[2048,768]{1,0:T(8,128)(2,1)}, f32[24,768]{1,0:T(8,128)}, f32[8,3072]{1,0:T(8,128)}) custom-call(s32[18]{0:T(128)} %stack.237.starts_ref, bf16[2048,768]{1,0:T(8,128)(2,1)} %get-tuple-element.53.dsec_ref.b_ref, bf16[2048,3072]{1,0:T(8,128)(2,1)} %get-tuple-element.54.slope_ref, ...), custom_call_target="tpu_custom_call" | custom-call | flops 21743271936 | bytes 49414144 | tf_op jit(solution)/shard_map/layer_backward/pallas_call | solution.py:451
  249.2 92.4 %attend_backward.1 = (bf16[2048,768]{1,0:T(8,128)(2,1)}, bf16[2048,768]{1,0:T(8,128)(2,1)}, bf16[2048,768]{1,0:T(8,128)(2,1)}) custom-call(s32[16]{0:T(128)} %get-tuple-element.126.low_ref, s32[16]{0:T(128)} %get-tuple-element.125.count_ref, bf16[2048,2304]{1,0:T(8,128)(2,1)} %project.1.q_ref.k_ref.v_ref, bf16[2048,2304]{1,0:T(8,128)(2,1)} %project.1.q_ref.k_ref.v_ref, ...), custom_call_target="tpu_custom_call" | custom-call | flops 30000001024 | bytes 30000000 | tf_op jit(solution)/shard_map/attend_backward/pallas_call | solution.py:224
  341.6 7.5 %grad_q.1 = (bf16[192,768]{1,0:T(8,128)(2,1)}, bf16[192,768]{1,0:T(8,128)(2,1)}, bf16[384,768]{1,0:T(8,128)(2,1)}) custom-call(s32[8]{0:T(128)} %stack.247.owner_ref, bf16[2048,768]{1,0:T(8,128)(2,1)} %bitcast.142, bf16[2048,768]{1,0:T(8,128)(2,1)} %get-tuple-element.60.dq_ref.b_ref), custom_call_target="tpu_custom_call" | custom-call | flops 2415919104 | bytes 7471104 | tf_op jit(solution)/shard_map/grad_q/pallas_call | solution.py:499
  353.6 7.2 %grad_v.1 = (bf16[192,768]{1,0:T(8,128)(2,1)}, bf16[192,768]{1,0:T(8,128)(2,1)}, bf16[384,768]{1,0:T(8,128)(2,1)}) custom-call(s32[8]{0:T(128)} %stack.247.owner_ref, bf16[2048,768]{1,0:T(8,128)(2,1)} %bitcast.143, bf16[2048,768]{1,0:T(8,128)(2,1)} %get-tuple-element.62.dv_ref.b_ref), custom_call_target="tpu_custom_call" | custom-call | flops 2415919104 | bytes 7471104 | tf_op jit(solution)/shard_map/grad_v/pallas_call | solution.py:499
  361.8 15.5 %grad_in.1 = (bf16[192,3072]{1,0:T(8,128)(2,1)}, bf16[192,3072]{1,0:T(8,128)(2,1)}, bf16[384,3072]{1,0:T(8,128)(2,1)}) custom-call(s32[8]{0:T(128)} %stack.247.owner_ref, bf16[2048,768]{1,0:T(8,128)(2,1)} %get-tuple-element.78.a_ref, bf16[2048,3072]{1,0:T(8,128)(2,1)} %get-tuple-element.79.b_ref), custom_call_target="tpu_custom_call" | custom-call | flops 9663676416 | bytes 20447232 | tf_op jit(solution)/shard_map/grad_in/pallas_call | solution.py:499
  381.7 7.2 %grad_out.1 = (bf16[192,768]{1,0:T(8,128)(2,1)}, bf16[192,768]{1,0:T(8,128)(2,1)}, bf16[384,768]{1,0:T(8,128)(2,1)}) custom-call(s32[8]{0:T(128)} %stack.247.owner_ref, bf16[2048,768]{1,0:T(8,128)(2,1)} %get-tuple-element.51.att_ref.o_ref.a_ref, bf16[2048,768]{1,0:T(8,128)(2,1)} %get-tuple-element.57.dbranch_ref.b_ref), custom_call_target="tpu_custom_call" | custom-call | flops 2415919104 | bytes 7471104 | tf_op jit(solution)/shard_map/grad_out/pallas_call | solution.py:499
  394.3 15.5 %input_grad.1 = bf16[2048,768]{1,0:T(8,128)(2,1)} custom-call(s32[6]{0:T(128)} %stack.238.starts_ref, bf16[2048,768]{1,0:T(8,128)(2,1)} %get-tuple-element.57.dbranch_ref.b_ref, bf16[2048,768]{1,0:T(8,128)(2,1)} %get-tuple-element.60.dq_ref.b_ref, bf16[2048,768]{1,0:T(8,128)(2,1)} %get-tuple-element.61.dk_ref.b_ref, ...), custom_call_target="tpu_custom_call" | custom-call | flops 7247757312 | bytes 19267584 | tf_op jit(solution)/shard_map/input_grad/pallas_call | solution.py:451
  410.4 7.4 %grad_k.1 = (bf16[192,768]{1,0:T(8,128)(2,1)}, bf16[192,768]{1,0:T(8,128)(2,1)}, bf16[384,768]{1,0:T(8,128)(2,1)}) custom-call(s32[8]{0:T(128)} %stack.247.owner_ref, bf16[2048,768]{1,0:T(8,128)(2,1)} %bitcast.144, bf16[2048,768]{1,0:T(8,128)(2,1)} %get-tuple-element.61.dk_ref.b_ref), custom_call_target="tpu_custom_call" | custom-call | flops 2415919104 | bytes 7471104 | tf_op jit(solution)/shard_map/grad_k/pallas_call | solution.py:499
  423.0 7.4 %collective-permute-done.49 = bf16[192,768]{1,0:T(8,128)(2,1)S(1)} collective-permute-done((bf16[192,768]{1,0:T(8,128)(2,1)S(1)}, bf16[192,768]{1,0:T(8,128)(2,1)S(1)}, u32[]{:S(2)}, u32[]{:S(2)}) %collective-permute-start.49) | collective-permute-done | bytes 294944 | tf_op jit(solution)/shard_map/ppermute | solution.py:524
  430.6 6.1 %collective-permute-done.23 = bf16[192,768]{1,0:T(8,128)(2,1)S(1)} collective-permute-done((bf16[192,768]{1,0:T(8,128)(2,1)S(1)}, bf16[192,768]{1,0:T(8,128)(2,1)S(1)}, u32[]{:S(2)}, u32[]{:S(2)}) %collective-permute-start.23) | collective-permute-done | bytes 294944 | tf_op jit(solution)/shard_map/ppermute | solution.py:524
  484.6 19.1 %collective-permute-done.63 = bf16[768,768]{1,0:T(8,128)(2,1)S(1)} collective-permute-done((bf16[768,768]{1,0:T(8,128)(2,1)S(1)}, bf16[768,768]{1,0:T(8,128)(2,1)S(1)}, u32[]{:S(2)}, u32[]{:S(2)}) %collective-permute-start.63) | collective-permute-done | bytes 1179680 | tf_op jit(solution)/shard_map/ppermute | solution.py:524
  505.7 14.2 %collective-permute-done.56 = bf16[192,3072]{1,0:T(8,128)(2,1)S(1)} collective-permute-done((bf16[192,3072]{1,0:T(8,128)(2,1)S(1)}, bf16[192,3072]{1,0:T(8,128)(2,1)S(1)}, u32[]{:S(2)}, u32[]{:S(2)}) %collective-permute-start.56) | collective-permute-done | bytes 1179680 | tf_op jit(solution)/shard_map/ppermute | solution.py:524
  525.4 8.7 %collective-permute-done.64 = bf16[384,768]{1,0:T(8,128)(2,1)S(1)} collective-permute-done((bf16[384,768]{1,0:T(8,128)(2,1)S(1)}, bf16[384,768]{1,0:T(8,128)(2,1)S(1)}, u32[]{:S(2)}, u32[]{:S(2)}) %collective-permute-start.64) | collective-permute-done | bytes 589856 | tf_op jit(solution)/shard_map/ppermute | solution.py:524
  545.4 11.8 %collective-permute-done.58 = bf16[48,3072]{1,0:T(8,128)(2,1)S(1)} collective-permute-done((bf16[48,3072]{1,0:T(8,128)(2,1)S(1)}, bf16[48,3072]{1,0:T(8,128)(2,1)S(1)}, u32[]{:S(2)}, u32[]{:S(2)}) %collective-permute-start.58) | collective-permute-done | bytes 294944 | tf_op jit(solution)/shard_map/ppermute | solution.py:524
  558.7 8.6 %collective-permute-done.59 = bf16[48,3072]{1,0:T(8,128)(2,1)S(1)} collective-permute-done((bf16[48,3072]{1,0:T(8,128)(2,1)S(1)}, bf16[48,3072]{1,0:T(8,128)(2,1)S(1)}, u32[]{:S(2)}, u32[]{:S(2)}) %collective-permute-start.59) | collective-permute-done | bytes 294944 | tf_op jit(solution)/shard_map/ppermute | solution.py:524
  (294 shorter events, 143.7 us)
Async XLA Ops:
  7.4 51.3 %collective-permute-start.2 = (bf16[192,2304]{1,0:T(8,128)(2,1)}, bf16[192,2304]{1,0:T(8,128)(2,1)}, u32[]{:S(2)}, u32[]{:S(2)}) collective-permute-start(bf16[192,2304]{1,0:T(8,128)(2,1)} %refs_0_.7), channel_id=1, source_target_pairs={{0,8},{8,0},{16,24},{24,16},{1,9},{9,1},{17,25},{25,17},{2,10},{10... | collective-permute-start | bytes 2654216 | tf_op jit(solution)/shard_map/ppermute | solution.py:524
  8.6 18.7 %collective-permute-start.3 = (bf16[96,2304]{1,0:T(8,128)(2,1)S(1)}, bf16[96,2304]{1,0:T(8,128)(2,1)S(1)}, u32[]{:S(2)}, u32[]{:S(2)}) collective-permute-start(bf16[96,2304]{1,0:T(8,128)(2,1)S(1)} %constant_dynamic-slice_fusion.15), channel_id=1, source_target_pairs={{0,16},{8,24},{16,0},{24,8},{1,17},{9,25},{17,1},{25,9},{2,18},{10... | collective-permute-start | bytes 1327112 | tf_op jit(solution)/shard_map/ppermute | solution.py:524
  11.5 22.3 %collective-permute-start.7 = (bf16[192,768]{1,0:T(8,128)(2,1)}, bf16[192,768]{1,0:T(8,128)(2,1)}, u32[]{:S(2)}, u32[]{:S(2)}) collective-permute-start(bf16[192,768]{1,0:T(8,128)(2,1)} %refs_0_.6), channel_id=1, source_target_pairs={{0,8},{8,0},{16,24},{24,16},{1,9},{9,1},{17,25},{25,17},{2,10},{10... | collective-permute-start | bytes 884744 | tf_op jit(solution)/shard_map/ppermute | solution.py:524
  33.3 24.5 %collective-permute-start.18 = (bf16[384,768]{1,0:T(8,128)(2,1)S(1)}, bf16[384,768]{1,0:T(8,128)(2,1)}, u32[]{:S(2)}, u32[]{:S(2)}) collective-permute-start(bf16[384,768]{1,0:T(8,128)(2,1)S(1)} %constant_dynamic-slice_fusion.12), channel_id=1, source_target_pairs={{0,16},{8,24},{16,0},{24,8},{1,17},{9,25},{17,1},{25,9},{2,18},{10... | collective-permute-start | bytes 1769480 | tf_op jit(solution)/shard_map/ppermute | solution.py:524
  35.3 22.4 %collective-permute-start.5 = (bf16[96,2304]{1,0:T(8,128)(2,1)S(1)}, bf16[96,2304]{1,0:T(8,128)(2,1)}, u32[]{:S(2)}, u32[]{:S(2)}) collective-permute-start(bf16[96,2304]{1,0:T(8,128)(2,1)S(1)} %collective-permute-done.3.refs_2_), channel_id=1, source_target_pairs={{0,8},{8,0},{16,24},{24,16},{1,9},{9,1},{17,25},{25,17},{2,10},{10... | collective-permute-start | bytes 1327112 | tf_op jit(solution)/shard_map/ppermute | solution.py:524
  48.1 84.5 %collective-permute-start.12 = (bf16[192,3072]{1,0:T(8,128)(2,1)S(1)}, bf16[192,3072]{1,0:T(8,128)(2,1)}, u32[]{:S(2)}, u32[]{:S(2)}) collective-permute-start(bf16[192,3072]{1,0:T(8,128)(2,1)S(1)} %copy-done.9), channel_id=1, source_target_pairs={{0,8},{8,0},{16,24},{24,16},{1,9},{9,1},{17,25},{25,17},{2,10},{10... | collective-permute-start | bytes 3538952 | tf_op jit(solution)/shard_map/ppermute | solution.py:524
  57.8 74.8 %collective-permute-start.17 = (bf16[768,768]{1,0:T(8,128)(2,1)}, bf16[768,768]{1,0:T(8,128)(2,1)S(1)}, u32[]{:S(2)}, u32[]{:S(2)}) collective-permute-start(bf16[768,768]{1,0:T(8,128)(2,1)} %refs_12_.3), channel_id=1, source_target_pairs={{0,8},{8,0},{16,24},{24,16},{1,9},{9,1},{17,25},{25,17},{2,10},{10... | collective-permute-start | bytes 3538952 | tf_op jit(solution)/shard_map/ppermute | solution.py:524
  59.0 27.5 %collective-permute-start.19 = (bf16[384,768]{1,0:T(8,128)(2,1)}, bf16[384,768]{1,0:T(8,128)(2,1)}, u32[]{:S(2)}, u32[]{:S(2)}) collective-permute-start(bf16[384,768]{1,0:T(8,128)(2,1)} %collective-permute-done.18.refs_14_), channel_id=1, source_target_pairs={{0,1},{1,0},{2,3},{3,2},{4,5},{5,4},{6,7},{7,6},{8,9},{9,8},{10,11... | collective-permute-start | bytes 1769480 | tf_op jit(solution)/shard_map/ppermute | solution.py:524
  74.4 58.2 %collective-permute-start.20 = (bf16[384,768]{1,0:T(8,128)(2,1)}, bf16[384,768]{1,0:T(8,128)(2,1)}, u32[]{:S(2)}, u32[]{:S(2)}) collective-permute-start(bf16[384,768]{1,0:T(8,128)(2,1)} %collective-permute-done.18.refs_14_), channel_id=1, source_target_pairs={{0,8},{8,0},{16,24},{24,16},{1,9},{9,1},{17,25},{25,17},{2,10},{10... | collective-permute-start | bytes 1769480 | tf_op jit(solution)/shard_map/ppermute | solution.py:524
  74.5 58.2 %collective-permute-start.16 = (bf16[96,3072]{1,0:T(8,128)(2,1)S(1)}, bf16[96,3072]{1,0:T(8,128)(2,1)}, u32[]{:S(2)}, u32[]{:S(2)}) collective-permute-start(bf16[96,3072]{1,0:T(8,128)(2,1)S(1)} %collective-permute-done.14.refs_9_), channel_id=1, source_target_pairs={{0,8},{8,0},{16,24},{24,16},{1,9},{9,1},{17,25},{25,17},{2,10},{10... | collective-permute-start | bytes 1769480 | tf_op jit(solution)/shard_map/ppermute | solution.py:524
  86.5 46.2 %collective-permute-start.21 = (bf16[384,768]{1,0:T(8,128)(2,1)}, bf16[384,768]{1,0:T(8,128)(2,1)}, u32[]{:S(2)}, u32[]{:S(2)}) collective-permute-start(bf16[384,768]{1,0:T(8,128)(2,1)} %collective-permute-done.19.refs_15_), channel_id=1, source_target_pairs={{0,8},{8,0},{16,24},{24,16},{1,9},{9,1},{17,25},{25,17},{2,10},{10... | collective-permute-start | bytes 1769480 | tf_op jit(solution)/shard_map/ppermute | solution.py:524
  360.7 112.1 %collective-permute-start.62 = (bf16[1536,768]{1,0:T(8,128)(2,1)}, bf16[1536,768]{1,0:T(8,128)(2,1)S(1)}, u32[]{:S(2)}, u32[]{:S(2)}) collective-permute-start(bf16[1536,768]{1,0:T(8,128)(2,1)} %get-tuple-element.85), channel_id=1, source_target_pairs={{0,8},{8,0},{16,24},{24,16},{1,9},{9,1},{17,25},{25,17},{2,10},{10... | collective-permute-start | bytes 7077896 | tf_op jit(solution)/shard_map/ppermute | solution.py:524
  377.3 97.5 %collective-permute-start.55 = (bf16[384,3072]{1,0:T(8,128)(2,1)}, bf16[384,3072]{1,0:T(8,128)(2,1)}, u32[]{:S(2)}, u32[]{:S(2)}) collective-permute-start(bf16[384,3072]{1,0:T(8,128)(2,1)} %get-tuple-element.81), channel_id=1, source_target_pairs={{0,8},{8,0},{16,24},{24,16},{1,9},{9,1},{17,25},{25,17},{2,10},{10... | collective-permute-start | bytes 7077896 | tf_op jit(solution)/shard_map/ppermute | solution.py:524
  388.9 31.1 %collective-permute-start.48 = (bf16[384,768]{1,0:T(8,128)(2,1)}, bf16[384,768]{1,0:T(8,128)(2,1)S(1)}, u32[]{:S(2)}, u32[]{:S(2)}) collective-permute-start(bf16[384,768]{1,0:T(8,128)(2,1)} %get-tuple-element.76), channel_id=1, source_target_pairs={{0,8},{8,0},{16,24},{24,16},{1,9},{9,1},{17,25},{25,17},{2,10},{10... | collective-permute-start | bytes 1769480 | tf_op jit(solution)/shard_map/ppermute | solution.py:524
  388.9 31.5 %collective-permute-start.22 = (bf16[384,768]{1,0:T(8,128)(2,1)}, bf16[384,768]{1,0:T(8,128)(2,1)S(1)}, u32[]{:S(2)}, u32[]{:S(2)}) collective-permute-start(bf16[384,768]{1,0:T(8,128)(2,1)} %get-tuple-element.64), channel_id=1, source_target_pairs={{0,8},{8,0},{16,24},{24,16},{1,9},{9,1},{17,25},{25,17},{2,10},{10... | collective-permute-start | bytes 1769480 | tf_op jit(solution)/shard_map/ppermute | solution.py:524
  389.5 20.3 %collective-permute-start.46 = (f32[4,2304]{1,0:T(4,128)S(1)}, f32[4,2304]{1,0:T(4,128)S(1)}, u32[]{:S(2)}, u32[]{:S(2)}) collective-permute-start(f32[4,2304]{1,0:T(4,128)S(1)} %add.300), channel_id=1, source_target_pairs={{0,2},{1,3},{2,0},{3,1},{4,6},{5,7},{6,4},{7,5},{8,10},{9,11},{10,... | collective-permute-start | bytes 110600 | tf_op jit(solution)/shard_map/ppermute | solution.py:524
  422.8 20.3 %collective-permute-start.30 = (bf16[192,768]{1,0:T(8,128)(2,1)S(1)}, bf16[192,768]{1,0:T(8,128)(2,1)S(1)}, u32[]{:S(2)}, u32[]{:S(2)}) collective-permute-start(bf16[192,768]{1,0:T(8,128)(2,1)S(1)} %add_convert_fusion.15), channel_id=1, source_target_pairs={{0,16},{8,24},{16,0},{24,8},{1,17},{9,25},{17,1},{25,9},{2,18},{10... | collective-permute-start | bytes 884744 | tf_op jit(solution)/shard_map/ppermute | solution.py:524
  474.8 28.9 %collective-permute-start.63 = (bf16[768,768]{1,0:T(8,128)(2,1)S(1)}, bf16[768,768]{1,0:T(8,128)(2,1)S(1)}, u32[]{:S(2)}, u32[]{:S(2)}) collective-permute-start(bf16[768,768]{1,0:T(8,128)(2,1)S(1)} %add_convert_fusion.1), channel_id=1, source_target_pairs={{0,16},{8,24},{16,0},{24,8},{1,17},{9,25},{17,1},{25,9},{2,18},{10... | collective-permute-start | bytes 3538952 | tf_op jit(solution)/shard_map/ppermute | solution.py:524
  477.4 42.5 %collective-permute-start.56 = (bf16[192,3072]{1,0:T(8,128)(2,1)S(1)}, bf16[192,3072]{1,0:T(8,128)(2,1)S(1)}, u32[]{:S(2)}, u32[]{:S(2)}) collective-permute-start(bf16[192,3072]{1,0:T(8,128)(2,1)S(1)} %add_convert_fusion.3), channel_id=1, source_target_pairs={{0,16},{8,24},{16,0},{24,8},{1,17},{9,25},{17,1},{25,9},{2,18},{10... | collective-permute-start | bytes 3538952 | tf_op jit(solution)/shard_map/ppermute | solution.py:524
  479.2 43.9 %collective-permute-start.41 = (bf16[48,768]{1,0:T(8,128)(2,1)S(1)}, bf16[48,768]{1,0:T(8,128)(2,1)S(1)}, u32[]{:S(2)}, u32[]{:S(2)}) collective-permute-start(bf16[48,768]{1,0:T(8,128)(2,1)S(1)} %add_convert_fusion.24), channel_id=1, source_target_pairs={{0,2},{1,3},{2,0},{3,1},{4,6},{5,7},{6,4},{7,5},{8,10},{9,11},{10,... | collective-permute-start | bytes 221192 | tf_op jit(solution)/shard_map/ppermute | solution.py:524
  480.9 87.8 %collective-permute-start.54 = (bf16[96,768]{1,0:T(8,128)(2,1)S(1)}, bf16[96,768]{1,0:T(8,128)(2,1)S(1)}, u32[]{:S(2)}, u32[]{:S(2)}) collective-permute-start(bf16[96,768]{1,0:T(8,128)(2,1)S(1)} %bitcast.101), channel_id=1, source_target_pairs={{0,1},{1,0},{2,3},{3,2},{4,5},{5,4},{6,7},{7,6},{8,9},{9,8},{10,11... | collective-permute-start | bytes 442376 | tf_op jit(solution)/shard_map/ppermute | solution.py:524
  483.1 40.9 %collective-permute-start.28 = (bf16[96,768]{1,0:T(8,128)(2,1)S(1)}, bf16[96,768]{1,0:T(8,128)(2,1)S(1)}, u32[]{:S(2)}, u32[]{:S(2)}) collective-permute-start(bf16[96,768]{1,0:T(8,128)(2,1)S(1)} %bitcast.107), channel_id=1, source_target_pairs={{0,1},{1,0},{2,3},{3,2},{4,5},{5,4},{6,7},{7,6},{8,9},{9,8},{10,11... | collective-permute-start | bytes 442376 | tf_op jit(solution)/shard_map/ppermute | solution.py:524
  503.7 40.0 %collective-permute-start.35 = (bf16[96,768]{1,0:T(8,128)(2,1)S(1)}, bf16[96,768]{1,0:T(8,128)(2,1)S(1)}, u32[]{:S(2)}, u32[]{:S(2)}) collective-permute-start(bf16[96,768]{1,0:T(8,128)(2,1)S(1)} %bitcast.103), channel_id=1, source_target_pairs={{0,1},{1,0},{2,3},{3,2},{4,5},{5,4},{6,7},{7,6},{8,9},{9,8},{10,11... | collective-permute-start | bytes 442376 | tf_op jit(solution)/shard_map/ppermute | solution.py:524
  524.0 33.4 %collective-permute-start.42 = (bf16[96,768]{1,0:T(8,128)(2,1)S(1)}, bf16[96,768]{1,0:T(8,128)(2,1)S(1)}, u32[]{:S(2)}, u32[]{:S(2)}) collective-permute-start(bf16[96,768]{1,0:T(8,128)(2,1)S(1)} %bitcast.105), channel_id=1, source_target_pairs={{0,1},{1,0},{2,3},{3,2},{4,5},{5,4},{6,7},{7,6},{8,9},{9,8},{10,11... | collective-permute-start | bytes 442376 | tf_op jit(solution)/shard_map/ppermute | solution.py:524
  (70 other events, 845.5 us)

commit v3 on v2

--- a/solution.py
+++ b/solution.py
@@ -100,13 +100,13 @@
 
 def attend_backward_kernel(
     pairs, tiles, low_ref, count_ref, q_ref, k_ref, v_ref, do_ref, o_ref, lse_ref, kseg_ref, qseg_ref,
-    dq_ref, dk_ref, dv_ref, dk_acc, dv_acc,
+    out_ref, dk_acc, dv_acc, *, first_pair,
 ):
-    group = pl.program_id(1)
-    block = pl.program_id(2)
+    block = pl.program_id(1)
     place = pl.program_id(0) * tiles + block
     low = low_ref[place]
     count = count_ref[place]
+    part = pairs * PAIR
     scale = 1.0 / math.sqrt(HEAD_DIM)
     scaled_rows = head_rows(scale)
     plain_rows = head_rows(1.0)
@@ -121,6 +121,7 @@
         chunks = [pl.ds(pl.multiple_of(start + c * TILE, TILE), TILE) for c in range(size)]
         whole = pl.ds(pl.multiple_of(start, TILE), size * TILE)
         masks = [kseg_ref[c, :] == qseg_ref[0] for c in chunks]
+        mine = pl.ds(pl.multiple_of(block * TILE, TILE), TILE)
         for p in range(pairs):
             lanes = slice(p * PAIR, (p + 1) * PAIR)
             queries = stack_heads(q_ref[:, lanes], scaled_rows)
@@ -134,16 +135,16 @@
                 ],
                 axis=1,
             )
-            lse = lse_ref[0, pl.ds(group * pairs + p, 1), :]
+            lse = lse_ref[0, first_pair + p : first_pair + p + 1, :]
             kept = []
             for c, mask in zip(chunks, masks):
-                part = dot_nt(k_ref[c, lanes], queries) - lse
+                part_scores = dot_nt(k_ref[c, lanes], queries) - lse
                 d_probs = dot_nt(v_ref[c, lanes], stacked)
                 probs = jnp.exp(
                     jnp.concatenate(
                         [
-                            jnp.where(mask, part[:, :TILE], masked_score),
-                            jnp.where(mask, part[:, TILE:], masked_score),
+                            jnp.where(mask, part_scores[:, :TILE], masked_score),
+                            jnp.where(mask, part_scores[:, TILE:], masked_score),
                         ],
                         axis=1,
                     )
@@ -153,14 +154,14 @@
                 dv_acc[c, lanes] += dot_nn(probs.astype(BF), stacked)
                 dk_acc[c, lanes] += dot_nn(d_scores, queries)
             mixed = dot_tn(k_ref[whole, lanes], jnp.concatenate(kept, axis=0)) * scale
-            dq_ref[:, lanes] = diagonal_back(mixed).astype(BF)
+            out_ref[mine, lanes] = diagonal_back(mixed).astype(BF)
 
     for_windows(count, tiles, window)
 
     @pl.when(block == tiles - 1)
     def _():
-        dk_ref[...] = dk_acc[...].astype(BF)
-        dv_ref[...] = dv_acc[...].astype(BF)
+        out_ref[:, part : 2 * part] = dk_acc[...].astype(BF)
+        out_ref[:, 2 * part :] = dv_acc[...].astype(BF)
 
 
 def windows_of(segments):
@@ -171,8 +172,9 @@
     last = blocked[:, :, TILE - 1]
     starts = jnp.sum((segments[:, None, :] < first[:, :, None]).astype(jnp.int32), axis=-1)
     ends = jnp.sum((segments[:, None, :] <= last[:, :, None]).astype(jnp.int32), axis=-1)
-    low = starts // TILE
-    count = (ends + TILE - 1) // TILE - low
+    bits = TILE.bit_length() - 1
+    low = lax.shift_right_logical(starts, bits)
+    count = lax.shift_right_logical(ends + TILE - 1, bits) - low
     key_ids = jnp.broadcast_to(segments.reshape(sequences * length, 1), (sequences * length, TILE))
     query_ids = blocked.reshape(sequences * tiles, 1, TILE)
     return low.reshape(-1), count.reshape(-1), key_ids, query_ids
@@ -207,12 +209,12 @@
             jax.ShapeDtypeStruct((sequences * tiles, 8, 2 * TILE), F32),
         ],
         compiler_params=pltpu.CompilerParams(vmem_limit_bytes=VMEM_LIMIT),
-        cost_estimate=pl.CostEstimate(flops=8 * 10**9, bytes_accessed=16 * 10**6, transcendentals=0),
+        cost_estimate=cost(8 * 10**9, 16 * 10**6),
         name="attend_forward",
     )(low, count, projected, projected, projected, key_ids, query_ids)
 
 
-def attend_backward(projected, d_attended, attended, lse, windows, sequences, groups=2):
+def attend_backward(projected, d_attended, attended, lse, windows, sequences, group, groups):
     low, count, key_ids, query_ids = windows
     rows = projected.shape[0]
     width = projected.shape[1] // 3
@@ -220,32 +222,28 @@
     tiles = length // TILE
     part = width // groups
     pairs = part // PAIR
-    query_spec = pl.BlockSpec((TILE, part), lambda s, g, b, *_: (s * tiles + b, g))
+    query_spec = pl.BlockSpec((TILE, part), lambda s, b, *_: (s * tiles + b, group))
     return pl.pallas_call(
-        functools.partial(attend_backward_kernel, pairs, tiles),
+        functools.partial(attend_backward_kernel, pairs, tiles, first_pair=group * pairs),
         grid_spec=pltpu.PrefetchScalarGridSpec(
             num_scalar_prefetch=2,
-            grid=(sequences, groups, tiles),
+            grid=(sequences, tiles),
             in_specs=[
                 query_spec,
-                pl.BlockSpec((length, part), lambda s, g, b, *_: (s, groups + g)),
-                pl.BlockSpec((length, part), lambda s, g, b, *_: (s, 2 * groups + g)),
+                pl.BlockSpec((length, part), lambda s, b, *_: (s, groups + group)),
+                pl.BlockSpec((length, part), lambda s, b, *_: (s, 2 * groups + group)),
                 query_spec,
                 query_spec,
-                pl.BlockSpec((1, 8, 2 * TILE), lambda s, g, b, *_: (s * tiles + b, 0, 0)),
-                pl.BlockSpec((length, TILE), lambda s, g, b, *_: (s, 0)),
-                pl.BlockSpec((1, 1, TILE), lambda s, g, b, *_: (s * tiles + b, 0, 0)),
+                pl.BlockSpec((1, 8, 2 * TILE), lambda s, b, *_: (s * tiles + b, 0, 0)),
+                pl.BlockSpec((length, TILE), lambda s, b, *_: (s, 0)),
+                pl.BlockSpec((1, 1, TILE), lambda s, b, *_: (s * tiles + b, 0, 0)),
             ],
-            out_specs=[
-                query_spec,
-                pl.BlockSpec((length, part), lambda s, g, b, *_: (s, g)),
-                pl.BlockSpec((length, part), lambda s, g, b, *_: (s, g)),
-            ],
+            out_specs=pl.BlockSpec((length, 3 * part), lambda s, b, *_: (s, 0)),
             scratch_shapes=[pltpu.VMEM((length, part), F32), pltpu.VMEM((length, part), F32)],
         ),
-        out_shape=[jax.ShapeDtypeStruct((rows, width), BF)] * 3,
+        out_shape=jax.ShapeDtypeStruct((rows, 3 * part), BF),
         compiler_params=pltpu.CompilerParams(vmem_limit_bytes=VMEM_LIMIT),
-        cost_estimate=pl.CostEstimate(flops=30 * 10**9, bytes_accessed=30 * 10**6, transcendentals=0),
+        cost_estimate=cost(30 * 10**9 // groups, 30 * 10**6 // groups),
         name="attend_backward",
     )(low, count, projected, projected, projected, d_attended, attended, lse, key_ids, query_ids)
 
@@ -380,18 +378,22 @@
     sums_ref[16:24, :] += fold_rows(d_branch.astype(F32))
 
 
-def input_grad_kernel(count, starts_ref, dbranch_ref, dq_ref, dk_ref, dv_ref, *refs):
-    pieces = refs[:count]
-    o_ref, weight, sems = refs[count:]
+def input_grad_kernel(count, groups, starts_ref, dbranch_ref, *refs):
+    grads = refs[:groups]
+    pieces = refs[groups : groups + count]
+    o_ref, weight, sems = refs[groups + count :]
 
     @pl.when(pl.program_id(0) == 0)
     def _():
         load_pieces(starts_ref, pieces, [weight] * count, sems)
 
-    width = dq_ref.shape[1]
+    width = dbranch_ref.shape[1]
+    part = width // groups
     total = dbranch_ref[...].astype(F32)
-    for n, ref in enumerate((dq_ref, dk_ref, dv_ref)):
-        total = total + dot_nt(ref[...], weight[:, n * width : (n + 1) * width])
+    for g, ref in enumerate(grads):
+        for n in range(3):
+            first = n * width + g * part
+            total = total + dot_nt(ref[:, n * part : (n + 1) * part], weight[:, first : first + part])
     o_ref[...] = total.astype(BF)
 
 
@@ -412,8 +414,10 @@
         keep_ref[...] = part
 
 
-def weight_grad_cols_kernel(slots, owner_ref, a_ref, b_ref, keep_ref, pass_ref, send_ref, held):
-    part = dot_tn(a_ref[...], b_ref[...]).astype(BF)
+def weight_grad_cols_kernel(slots, owner_ref, a_ref, b_ref, keep_ref, pass_ref, send_ref, sums_ref, held):
+    terms = b_ref[...]
+    sums_ref[...] = fold_rows(terms.astype(F32))
+    part = dot_tn(a_ref[...], terms).astype(BF)
     height = keep_ref.shape[0]
     for owner in range(4):
         held[owner_ref[owner]] = part[owner * height : (owner + 1) * height]
@@ -427,7 +431,7 @@
 
 
 def cost(flops, bytes_accessed):
-    return pl.CostEstimate(flops=int(flops), bytes_accessed=int(bytes_accessed), transcendentals=0)
+    return pl.CostEstimate(flops=int(flops) // 16, bytes_accessed=int(bytes_accessed) // 16, transcendentals=0)
 
 
 def whole_spec(array):
@@ -509,10 +513,16 @@
                 pl.BlockSpec((part, block), lambda t, s: (0, t)),
                 pl.BlockSpec((part, block), lambda t, s: (0, t)),
                 pl.BlockSpec((2 * part, block), lambda t, s: (0, t)),
+                pl.BlockSpec((8, block), lambda t, s: (0, t)),
             ],
             scratch_shapes=[pltpu.VMEM((4, part, block), BF)],
         ),
-        out_shape=[shaped(part, width), shaped(part, width), shaped(2 * part, width)],
+        out_shape=[
+            shaped(part, width),
+            shaped(part, width),
+            shaped(2 * part, width),
+            shaped(8, width, dtype=F32),
+        ],
         compiler_params=PARAMS,
         cost_estimate=cost(flops, moved),
         name=name,
@@ -524,56 +534,90 @@
     return lax.ppermute(array, axis, [(i, i ^ bit) for i in range(size)])
 
 
-def gather_pieces(shard):
+def gather_hops(shards):
+    side = lax.axis_index("rep") & 1
+    halves = [s.shape[0] // 2 for s in shards]
+    mine = [lax.dynamic_slice_in_dim(s, side * h, h, axis=0) for s, h in zip(shards, halves)]
+    direct, core = yield [swap(m, "shard", 2) for m in mine], [swap(s, "shard", 1) for s in shards]
+    relayed, cross = yield [swap(d, "rep", 1) for d in direct], [swap(d, "shard", 1) for d in direct]
+    cross_relayed = yield [swap(r, "shard", 1) for r in relayed]
+    return [list(p) for p in zip(shards, core, direct, relayed, cross, cross_relayed)]
+
+
+def piece_starts(shard):
     height = shard.shape[0]
-    if lax.axis_size("shard") != 4 or lax.axis_size("rep") % 2:
-        return [(lax.all_gather(shard, "shard", axis=0, tiled=True), jnp.int32(0))]
     me = lax.axis_index("shard")
-    side = lax.rem(lax.axis_index("rep"), 2)
+    side = lax.axis_index("rep") & 1
     half = height // 2
-    mine = lax.dynamic_slice_in_dim(shard, side * half, half, axis=0)
-    direct = swap(mine, "shard", 2)
-    relayed = swap(direct, "rep", 1)
-    near = me * height
-    core = (me ^ 1) * height
-    far = (me ^ 2) * height
-    cross = (me ^ 3) * height
-    return [
-        (shard, near),
-        (swap(shard, "shard", 1), core),
-        (direct, far + side * half),
-        (relayed, far + (1 - side) * half),
-        (swap(direct, "shard", 1), cross + side * half),
-        (swap(relayed, "shard", 1), cross + (1 - side) * half),
-    ]
+    near, core, far, cross = [(me ^ o) * height for o in range(4)]
+    return [near, core, far + side * half, far + (1 - side) * half, cross + side * half, cross + (1 - side) * half]
 
 
 def added(*terms):
     return functools.reduce(jnp.add, [t.astype(F32) for t in terms]).astype(BF)
 
 
-def reduce_owned(parts):
+def reduce_hops(parts):
     keep, passed, sent = parts
     height = keep.shape[0]
-    come = swap(sent, "shard", 1)
-    onward = swap(added(passed, come[height:]), "shard", 2)
+    come = yield swap(sent, "shard", 1)
+    onward = yield swap(added(passed, come[height:]), "shard", 2)
     owned = added(keep, come[:height], onward)
     place = lax.axis_index("rep")
     half, quarter = height // 2, height // 4
-    y = lax.rem(place, 2)
-    z = lax.rem(place // 2, 2)
+    y = place & 1
+    z = lax.shift_right_logical(place, 1) & 1
     away = lax.dynamic_slice_in_dim(owned, (1 - y) * half, half, axis=0)
     stay = lax.dynamic_slice_in_dim(owned, y * half, half, axis=0)
-    stay = added(stay, swap(away, "rep", 1))
+    stay = added(stay, (yield swap(away, "rep", 1)))
     away = lax.dynamic_slice_in_dim(stay, (1 - z) * quarter, quarter, axis=0)
     stay = lax.dynamic_slice_in_dim(stay, z * quarter, quarter, axis=0)
-    stay = added(stay, swap(away, "rep", 2))
-    stay = added(stay, swap(stay, "rep", 4))
-    other = swap(stay, "rep", 2)
+    stay = added(stay, (yield swap(away, "rep", 2)))
+    stay = added(stay, (yield swap(stay, "rep", 4)))
+    other = yield swap(stay, "rep", 2)
     pair = jnp.where(z == 0, jnp.stack([stay, other]), jnp.stack([other, stay])).reshape(half, -1)
-    other = swap(pair, "rep", 1)
+    other = yield swap(pair, "rep", 1)
     both = jnp.where(y == 0, jnp.stack([pair, other]), jnp.stack([other, pair])).reshape(height, -1)
     return both.astype(F32)
+
+
+def reduce_small(packed):
+    for axis, bit in (("shard", 1), ("shard", 2), ("rep", 1), ("rep", 2), ("rep", 4)):
+        packed = packed + (yield swap(packed, axis, bit))
+    return packed
+
+
+class Flow:
+    def __init__(self, hops):
+        self.hops = hops
+        self.result = None
+        self.flying = next(hops)
+
+    def land(self, arrived):
+        try:
+            self.flying = self.hops.send(arrived)
+        except StopIteration as stop:
+            self.flying, self.result = None, stop.value
+
+
+class Line:
+    def __init__(self):
+        self.flows = []
+        self.recent = []
+
+    def step(self, arrays, flows=None):
+        moving = [f for f in (self.flows if flows is None else flows) if f.flying is not None]
+        held = self.recent
+        arrays, arrived, held = lax.optimization_barrier((arrays, [f.flying for f in moving], held))
+        for flow, value in zip(moving, arrived):
+            flow.land(value)
+        self.recent = []
+        return arrays
+
+    def start(self, hops):
+        flow = Flow(hops)
+        self.flows.append(flow)
+        return flow
 
 
 def reduce_plain(a, b):
@@ -612,54 +656,63 @@
     direct = group == 4 and lax.axis_size("rep") == 8
 
     part = b_query.shape[0]
+    line = Line()
     small_shards = (b_query, b_value, b_out, gain_one, shift_one, b_ffo, gain_two, shift_two, b_in)
     small = jnp.concatenate(small_shards).reshape(1, -1)
     if direct:
+        qkv_flow = Flow(gather_hops([w_qkv]))
         near = swap(small, "shard", 1)
         pair = jnp.concatenate([small, near], axis=0)
         four = jnp.concatenate([pair, swap(pair, "shard", 2)], axis=0)
         order = [jnp.bitwise_xor(me, o) for o in range(4)]
         small_full = jnp.concatenate([lax.dynamic_slice_in_dim(four, o, 1, axis=0) for o in order], axis=0)
+        later = line.step([w_out, w_in, w_ffo], [qkv_flow])
+        later_flow = Flow(gather_hops(later))
+        seg = line.step(seg, [qkv_flow])
+        x_first = line.step(x, [qkv_flow])
+        (qkv_pieces,) = qkv_flow.result
+        qkv_starts = jnp.stack(piece_starts(w_qkv)).astype(jnp.int32)
+        layer_starts = jnp.stack(sum([piece_starts(w) for w in (w_out, w_in, w_ffo)], [])).astype(jnp.int32)
+        counts = (6, 6, 6)
     else:
         small_full = lax.all_gather(small, "shard", axis=0, tiled=True)
+        qkv_pieces, *layer_lists = [
+            [lax.all_gather(w, "shard", axis=0, tiled=True)] for w in (w_qkv, w_out, w_in, w_ffo)
+        ]
+        x_first = x
+        qkv_starts = jnp.zeros((1,), jnp.int32)
+        layer_starts = jnp.zeros((3,), jnp.int32)
+        counts = (1, 1, 1)
     small_full = small_full.astype(F32)
     vectors = [small_full[:, i * part : (i + 1) * part].reshape(1, -1) for i in range(8)]
     bias_all = jnp.concatenate([vectors[0], jnp.zeros_like(vectors[0]), vectors[1]], axis=1)
     vec = jnp.concatenate(vectors[2:] + [jnp.zeros((2, width), F32)], axis=0)
     bias_in = small_full[:, 8 * part :].reshape(1, -1)
 
-    qkv_pieces = gather_pieces(w_qkv)
-    out_pieces = gather_pieces(w_out)
-    in_pieces = gather_pieces(w_in)
-    ffo_pieces = gather_pieces(w_ffo)
-
-    def arrays(pieces):
-        return [p[0] for p in pieces]
-
-    def starts(pieces):
-        return jnp.stack([jnp.asarray(p[1], jnp.int32) for p in pieces])
-
     windows = windows_of(seg)
     block = 256
-    qkv_starts = starts(qkv_pieces)
     (projected,) = row_call(
         functools.partial(project_kernel, len(qkv_pieces)),
         "project",
         rows,
         block,
         qkv_starts,
-        [x],
+        [x_first],
         [bias_all],
-        arrays(qkv_pieces),
+        qkv_pieces,
         [shaped(rows, 3 * width)],
         [],
         [pltpu.VMEM((width, 3 * width), BF)],
         6 * rows * width * width,
     )
+    if direct:
+        projected = line.step(projected, [later_flow])
     attended, lse = attend_forward(projected, windows, total)
-    layer_pieces = out_pieces + in_pieces + ffo_pieces
-    counts = (len(out_pieces), len(in_pieces), len(ffo_pieces))
-    layer_starts = starts(layer_pieces)
+    if direct:
+        attended = line.step(attended, [later_flow])
+        attended = line.step(attended, [later_flow])
+        layer_lists = later_flow.result
+    layer_pieces = sum(layer_lists, [])
     weights_scratch = [
         pltpu.VMEM((width, width), BF),
         pltpu.VMEM((width, hidden_width), BF),
@@ -674,7 +727,7 @@
         layer_starts,
         [x, attended, cot],
         [vec, bias_in],
-        arrays(layer_pieces),
+        layer_pieces,
         [
             shaped(rows, width),
             shaped(rows, width),
@@ -691,15 +744,19 @@
 
     place = [jnp.bitwise_xor(me, o) for o in range(4)]
     slots = jnp.stack(
-        [(p % 2) * 2 + p // 2 for p in place] + [jnp.bitwise_xor(me, j) for j in (1, 3, 2, 0)]
+        [(p & 1) * 2 + lax.shift_right_logical(p, 1) for p in place] + [jnp.bitwise_xor(me, j) for j in (1, 3, 2, 0)]
     ).astype(jnp.int32)
 
     def weight_terms(a, b, name):
         if direct:
-            return reduce_owned(weight_grad(slots, a, b, name))
-        return reduce_plain(a, b)
-
-    grad_ffo = weight_terms(hidden, d_second, "grad_ffo")
+            terms = weight_grad(slots, a, b, name)
+            line.recent.append(terms[0])
+            return line.start(reduce_hops(terms[:3])), terms[3:]
+        return reduce_plain(a, b), [fold_rows(b.astype(F32))]
+
+    flow_ffo, _ = weight_terms(hidden, d_second, "grad_ffo")
+    if direct:
+        d_second, layer_pieces = line.step((d_second, layer_pieces), [])
     d_pre, d_branch, d_attended, sums_one, sums_in = row_call(
         functools.partial(layer_backward_kernel, counts),
         "layer_backward",
@@ -708,34 +765,30 @@
         layer_starts,
         [d_second, slope, n_one, rstd_one],
         [vec],
-        arrays(layer_pieces),
+        layer_pieces,
         [shaped(rows, hidden_width), shaped(rows, width), shaped(rows, width)],
         [shaped(24, width, dtype=F32), shaped(8, hidden_width, dtype=F32)],
         weights_scratch,
         layer_flops,
     )
-    grad_in = weight_terms(normed, d_pre, "grad_in")
-    grad_out = weight_terms(attended, d_branch, "grad_out")
-    dq, dk, dv = attend_backward(projected, d_attended, attended, lse, windows, total)
-    grad_q = weight_terms(x, dq, "grad_q")
-    grad_k = weight_terms(x, dk, "grad_k")
-    grad_v = weight_terms(x, dv, "grad_v")
-    (d_tokens,) = row_call(
-        functools.partial(input_grad_kernel, len(qkv_pieces)),
-        "input_grad",
-        rows,
-        block,
-        qkv_starts,
-        [d_branch, dq, dk, dv],
-        [],
-        arrays(qkv_pieces),
-        [shaped(rows, width)],
-        [],
-        [pltpu.VMEM((width, 3 * width), BF)],
-        6 * rows * width * width,
-    )
-    d_query_bias = jnp.sum(dq.astype(F32), axis=0)
-    d_value_bias = jnp.sum(dv.astype(F32), axis=0)
+    if direct:
+        d_pre, d_branch, d_attended = line.step((d_pre, d_branch, d_attended))
+    flow_in, _ = weight_terms(normed, d_pre, "grad_in")
+    if direct:
+        d_branch, d_attended = line.step((d_branch, d_attended), [])
+    flow_out, _ = weight_terms(attended, d_branch, "grad_out")
+    groups = 3
+    d_heads, flows, head_sums = [], [], []
+    for g in range(groups):
+        if direct:
+            d_attended = line.step(d_attended)
+        d_head = attend_backward(projected, d_attended, attended, lse, windows, total, g, groups)
+        if direct:
+            d_head = line.step(d_head)
+        flow, sums = weight_terms(x, d_head, "grad_qkv")
+        d_heads.append(d_head)
+        flows.append(flow)
+        head_sums.append(sums[0])
 
     def folded(sums):
         return [jnp.sum(sums[i : i + 8], axis=0) for i in range(0, sums.shape[0], 8)]
@@ -743,16 +796,41 @@
     d_gain_two, d_shift_two, d_ffo_bias = folded(sums_two)
     d_gain_one, d_shift_one, d_out_bias = folded(sums_one)
     (d_in_bias,) = folded(sums_in)
+    cut = width // groups
+    head_sums = [jnp.sum(s, axis=0) for s in head_sums]
+    d_query_bias = jnp.concatenate([s[:cut] for s in head_sums])
+    d_value_bias = jnp.concatenate([s[2 * cut :] for s in head_sums])
     smalls = (
         d_query_bias, d_value_bias, d_out_bias, d_gain_one, d_shift_one, d_ffo_bias, d_gain_two, d_shift_two,
         d_in_bias,
     )
     packed = jnp.concatenate([s.reshape(group, -1) for s in smalls], axis=1)
     if direct:
-        for axis, bit in (("shard", 1), ("shard", 2), ("rep", 1), ("rep", 2), ("rep", 4)):
-            packed = packed + swap(packed, axis, bit)
+        flow_small = line.start(reduce_small(packed))
+        d_branch = line.step(d_branch, [])
+    (d_tokens,) = row_call(
+        functools.partial(input_grad_kernel, len(qkv_pieces), groups),
+        "input_grad",
+        rows,
+        block,
+        qkv_starts,
+        [d_branch, *d_heads],
+        [],
+        qkv_pieces,
+        [shaped(rows, width)],
+        [],
+        [pltpu.VMEM((width, 3 * width), BF)],
+        6 * rows * width * width,
+    )
+    if direct:
+        while any(f.flying is not None for f in line.flows):
+            d_tokens = line.step(d_tokens)
+        packed = flow_small.result
+        grad_ffo, grad_in, grad_out, *grads = [f.result for f in (flow_ffo, flow_in, flow_out, *flows)]
     else:
         packed = lax.psum(packed, ("shard", "rep"))
+        grad_ffo, grad_in, grad_out, grads = flow_ffo, flow_in, flow_out, flows
+    grad_qkv = jnp.concatenate([g[:, n * cut : (n + 1) * cut] for n in range(3) for g in grads], axis=1)
     mine = lax.dynamic_index_in_dim(packed, me, 0, keepdims=False)
     sm = [mine[i * part : (i + 1) * part] for i in range(8)]
     gqb, gvb, gob, gg1, gs1, gfb, gg2, gs2 = sm
@@ -760,7 +838,7 @@
     return (
         output.reshape(tokens.shape),
         d_tokens.reshape(tokens.shape),
-        jnp.concatenate([grad_q, grad_k, grad_v], axis=1),
+        grad_qkv,
         gqb,
         gvb,
         grad_out,

time: 600 us -> 557 us (0.928)
  waiting for transfers between devices: 156 us -> 83 us
  local copies, waits for them, and re-layouts: 18.6 us -> 36.5 us
  Pallas kernels: 327 us -> 340 us
  other arithmetic: 18.2 us -> 28 us
    ppermute x69, waiting for transfers between devices: 156 us -> 83 us  [swap(): return lax.ppermute(array, axis, [(i, i ^ bit) for i in range(size)])]
    pallas_call x1 -> x3, Pallas kernels: 92.4 us -> 104 us  [attend_backward(): pl.pallas_call(functools.partial(attend_backward_kernel, pairs, tiles, fi...]
    convert_element_type x30, other arithmetic: 6 us -> 15.3 us  [added(): return functools.reduce(jnp.add, [t.astype(F32) for t in terms]).astype(BF)]
    unnamed x55 -> x119, local copies, waits for them, and re-layouts: 2.18 us -> 8.31 us
  transfers between devices with their start and end apart: 69 -> 69, of which waited for: 27 -> 24; matrix products, arithmetic and copies ran while one was open for 4% -> 8% of each run, Pallas kernels for 19% -> 45%
where the time goes in v3:
time: 557 us; the launch traced here: 550 us
  Pallas kernels  340 us (61%)
  waiting for transfers between devices  83 us (15%)
  starting transfers between devices  61.1 us (11%)
  local copies, waits for them, and re-layouts  36.5 us (7%)
  other arithmetic  28 us (5%)
    pallas_call x4, Pallas kernels, row_call(): pl.pallas_call(kernel, grid_spec=pltpu.PrefetchScalarGridSpec(num_scalar_...  129 us
    pallas_call x3, Pallas kernels, attend_backward(): pl.pallas_call(functools.partial(attend_backward_kernel, pairs, tiles, fi...  104 us
    ppermute x69, waiting for transfers between devices, swap(): return lax.ppermute(array, axis, [(i, i ^ bit) for i in range(size)])  83 us
    ppermute x69, starting transfers between devices, swap(): return lax.ppermute(array, axis, [(i, i ^ bit) for i in range(size)])  61.1 us
    pallas_call x5, Pallas kernels, weight_grad(): pl.pallas_call(functools.partial(weight_grad_cols_kernel, 4), grid_spec=p...  45 us
    pallas_call x1, Pallas kernels, attend_forward(): pl.pallas_call(functools.partial(attend_forward_kernel, pairs, tiles), gr...  44.6 us
    pallas_call x1, Pallas kernels, weight_grad(): pl.pallas_call(weight_grad_rows_kernel, grid_spec=pltpu.PrefetchScalarGri...  16.5 us
    convert_element_type x30, other arithmetic, added(): return functools.reduce(jnp.add, [t.astype(F32) for t in terms]).astype(BF)  15.3 us
  transfers between devices with their start and end apart: 69, of which 24 were waited for; matrix products, arithmetic and copies ran while one was open for 8% of the time, Pallas kernels for 45%

profile of v3, /device:TPU:0, one launch (start us, length us, event | category | flops | bytes accessed | tf_op | source)
XLA Modules:
  0.0 550.3 jit_solution(17366270730223229349)
XLA Ops:
  0.7 6.3 %concatenate.31 = bf16[2304]{0:T(1024)(128)(2,1)S(1)} concatenate(bf16[192]{0:T(256)(128)(2,1)} %param.20, bf16[192]{0:T(256)(128)(2,1)} %param.21, bf16[192]{0:T(256)(128)(2,1)} %param.23, bf16[192]{0:T(256)(128)(2,1)} %param.24, bf16[192]{0:T(256)(128)(2,1)} %param.25, bf16[192]{0:T(256)(128)(2,1)} %param.29, bf16[192]{0:T(256)(128)(2,1)} %param.30, bf16[192]{0:T(256)(128)(2,1)} %param.31, ...), dimensions={0} | concatenate | bytes 9216 | tf_op jit(solution)/shard_map/concatenate | solution.py:661
  15.1 10.2 %collective-permute-done.refs_2_.refs_5_ = bf16[96,2304]{1,0:T(8,128)(2,1)} collective-permute-done((bf16[96,2304]{1,0:T(8,128)(2,1)}, bf16[96,2304]{1,0:T(8,128)(2,1)}, u32[]{:S(2)}, u32[]{:S(2)}) %collective-permute-start) | collective-permute-done | bytes 442400 | tf_op jit(solution)/shard_map/ppermute | solution.py:534
  30.1 8.1 %collective-permute-done.2.refs_3_.refs_6_ = bf16[96,2304]{1,0:T(8,128)(2,1)} collective-permute-done((bf16[96,2304]{1,0:T(8,128)(2,1)}, bf16[96,2304]{1,0:T(8,128)(2,1)}, u32[]{:S(2)}, u32[]{:S(2)}) %collective-permute-start.2) | collective-permute-done | bytes 442400 | tf_op jit(solution)/shard_map/ppermute | solution.py:534
  42.8 14.3 %project.1.q_ref.k_ref.v_ref = bf16[2048,2304]{1,0:T(8,128)(2,1)} custom-call(s32[6]{0:T(128)} %stack.238.starts_ref, bf16[2048,768]{1,0:T(8,128)(2,1)} %bitcast.101, f32[1,2304]{1,0:T(1,128)} %fusion.bias_ref, bf16[192,2304]{1,0:T(8,128)(2,1)} %refs_3_.1, bf16[192,2304]{1,0:T(8,128)(2,1)} %copy-done.3, ...), custom_call_target="tpu_custom_call" | custom-call | flops 452984832 | bytes 1007616 | tf_op jit(solution)/shard_map/project/pallas_call | solution.py:455
  57.1 11.4 %collective-permute-done.8.refs_8_ = bf16[96,3072]{1,0:T(8,128)(2,1)S(1)} collective-permute-done((bf16[96,3072]{1,0:T(8,128)(2,1)}, bf16[96,3072]{1,0:T(8,128)(2,1)S(1)}, u32[]{:S(2)}, u32[]{:S(2)}) %collective-permute-start.8) | collective-permute-done | bytes 589856 | tf_op jit(solution)/shard_map/ppermute | solution.py:534
  79.0 44.6 %attend_forward.1 = (bf16[2048,768]{1,0:T(8,128)(2,1)}, f32[16,8,256]{2,1,0:T(8,128)}) custom-call(s32[16]{0:T(128)} %copy-done.50, s32[16]{0:T(128)} %sub.14.count_ref, bf16[2048,2304]{1,0:T(8,128)(2,1)} %project.1.q_ref.k_ref.v_ref, bf16[2048,2304]{1,0:T(8,128)(2,1)} %project.1.q_ref.k_ref.v_ref, bf16[2048,2304]{1,0:T(8,128)(2,1)} %project.1.q_ref.k_ref.v_ref, ...), custom_call_target="tpu_custom_call" | custom-call | flops 500000000 | bytes 1000000 | tf_op jit(solution)/shard_map/attend_forward/pallas_call | solution.py:190
  130.6 59.4 %layer_forward.1 = (bf16[2048,768]{1,0:T(8,128)(2,1)}, bf16[2048,768]{1,0:T(8,128)(2,1)}, bf16[2048,768]{1,0:T(8,128)(2,1)}, f32[2048,128]{1,0:T(8,128)}, bf16[2...) custom-call(s32[18]{0:T(128)} %stack.237.starts_ref, ...), custom_call_target="tpu_custom_call" | custom-call | flops 1358954496 | bytes 3678208 | tf_op jit(solution)/shard_map/layer_forward/pallas_call | solution.py:455
  190.0 16.5 %grad_ffo.1 = (bf16[768,768]{1,0:T(8,128)(2,1)}, bf16[768,768]{1,0:T(8,128)(2,1)}, bf16[1536,768]{1,0:T(8,128)(2,1)}) custom-call(s32[8]{0:T(128)} %stack.247.owner_ref, bf16[2048,3072]{1,0:T(8,128)(2,1)} %get-tuple-element.195.a_ref, bf16[2048,768]{1,0:T(8,128)(2,1)} %get-tuple-element.197.b_ref.dsec_ref), custom_call_target="tpu_custom_call" | custom-call | flops 603979776 | bytes 1277952 | tf_op jit(solution)/shard_map/grad_ffo/pallas_call | solution.py:482
  207.0 40.0 %layer_backward.1 = (bf16[2048,3072]{1,0:T(8,128)(2,1)}, bf16[2048,768]{1,0:T(8,128)(2,1)}, bf16[2048,768]{1,0:T(8,128)(2,1)}, f32[24,768]{1,0:T(8,128)}, f32[8,3072]{1,0:T(8,128)}) custom-call(s32[18]{0:T(128)} %stack.237.starts_ref, bf16[2048,768]{1,0:T(8,128)(2,1)} %get-tuple-element.197.b_ref.dsec_ref, bf16[2048,3072]{1,0:T(8,128)(2,1)} %get-tuple-element.198.slope_ref, ...), custom_call_target="tpu_custom_call" | custom-call | flops 1358954496 | bytes 3088384 | tf_op jit(solution)/shard_map/layer_backward/pallas_call | solution.py:455
  247.0 16.0 %grad_in.1 = (bf16[192,3072]{1,0:T(8,128)(2,1)}, bf16[192,3072]{1,0:T(8,128)(2,1)}, bf16[384,3072]{1,0:T(8,128)(2,1)}, f32[8,3072]{1,0:T(8,128)}) custom-call(s32[8]{0:T(128)} %stack.247.owner_ref, bf16[2048,768]{1,0:T(8,128)(2,1)} %get-tuple-element.225.a_ref, bf16[2048,3072]{1,0:T(8,128)(2,1)} %get-tuple-element.226.b_ref), custom_call_target="tpu_custom_call" | custom-call | flops 603979776 | bytes 1277952 | tf_op jit(solution)/shard_map/grad_in/pallas_call | solution.py:503
  267.0 7.3 %grad_out.1 = (bf16[192,768]{1,0:T(8,128)(2,1)}, bf16[192,768]{1,0:T(8,128)(2,1)}, bf16[384,768]{1,0:T(8,128)(2,1)}, f32[8,768]{1,0:T(8,128)}) custom-call(s32[8]{0:T(128)} %stack.247.owner_ref, bf16[2048,768]{1,0:T(8,128)(2,1)} %get-tuple-element.183.att_ref.a_ref.o_ref, bf16[2048,768]{1,0:T(8,128)(2,1)} %get-tuple-element.270.b_ref.dbranch_ref), custom_call_target="tpu_custom_call" | custom-call | flops 150994944 | bytes 466944 | tf_op jit(solution)/shard_map/grad_out/pallas_call | solution.py:503
  276.6 17.7 %collective-permute-done.23 = bf16[768,768]{1,0:T(8,128)(2,1)} collective-permute-done((bf16[768,768]{1,0:T(8,128)(2,1)}, bf16[768,768]{1,0:T(8,128)(2,1)}, u32[]{:S(2)}, u32[]{:S(2)}) %collective-permute-start.23) | collective-permute-done | bytes 1179680 | tf_op jit(solution)/shard_map/ppermute | solution.py:534
  301.6 34.7 %attend_backward.3.b_ref.refs_0_ = bf16[2048,768]{1,0:T(8,128)(2,1)} custom-call(s32[16]{0:T(128)} %copy-done.50, s32[16]{0:T(128)} %sub.14.count_ref, bf16[2048,2304]{1,0:T(8,128)(2,1)} %project.1.q_ref.k_ref.v_ref, bf16[2048,2304]{1,0:T(8,128)(2,1)} %project.1.q_ref.k_ref.v_ref, bf16[2048,2304]{1,0:T(8,128)(2,1)} %project.1.q_ref.k_ref.v_ref, ...), custom_call_target="tpu_custom_call" | custom-call | flops 625000000 | bytes 625000 | tf_op jit(solution)/shard_map/attend_backward/pallas_call | solution.py:226
  341.2 7.3 %grad_qkv.3 = (bf16[192,768]{1,0:T(8,128)(2,1)}, bf16[192,768]{1,0:T(8,128)(2,1)}, bf16[384,768]{1,0:T(8,128)(2,1)}, f32[8,768]{1,0:T(8,128)}) custom-call(s32[8]{0:T(128)} %stack.247.owner_ref, bf16[2048,768]{1,0:T(8,128)(2,1)} %bitcast.103, bf16[2048,768]{1,0:T(8,128)(2,1)} %attend_backward.3.b_ref.refs_0_), custom_call_target="tpu_custom_call" | custom-call | flops 150994944 | bytes 466944 | tf_op jit(solution)/shard_map/grad_qkv/pallas_call | solution.py:503
  353.7 5.2 collective-permute-done.31
  374.2 35.0 %attend_backward.4.b_ref.refs_1_ = bf16[2048,768]{1,0:T(8,128)(2,1)} custom-call(s32[16]{0:T(128)} %copy-done.50, s32[16]{0:T(128)} %sub.14.count_ref, bf16[2048,2304]{1,0:T(8,128)(2,1)} %project.1.q_ref.k_ref.v_ref, bf16[2048,2304]{1,0:T(8,128)(2,1)} %project.1.q_ref.k_ref.v_ref, bf16[2048,2304]{1,0:T(8,128)(2,1)} %project.1.q_ref.k_ref.v_ref, ...), custom_call_target="tpu_custom_call" | custom-call | flops 625000000 | bytes 625000 | tf_op jit(solution)/shard_map/attend_backward/pallas_call | solution.py:226
  413.2 7.2 %grad_qkv.4 = (bf16[192,768]{1,0:T(8,128)(2,1)}, bf16[192,768]{1,0:T(8,128)(2,1)}, bf16[384,768]{1,0:T(8,128)(2,1)}, f32[8,768]{1,0:T(8,128)}) custom-call(s32[8]{0:T(128)} %stack.247.owner_ref, bf16[2048,768]{1,0:T(8,128)(2,1)} %bitcast.104, bf16[2048,768]{1,0:T(8,128)(2,1)} %attend_backward.4.b_ref.refs_1_), custom_call_target="tpu_custom_call" | custom-call | flops 150994944 | bytes 466944 | tf_op jit(solution)/shard_map/grad_qkv/pallas_call | solution.py:503
  423.9 3.2 collective-permute-done.40
  434.2 34.7 %attend_backward.5.b_ref.refs_2_ = bf16[2048,768]{1,0:T(8,128)(2,1)} custom-call(s32[16]{0:T(128)} %copy-done.50, s32[16]{0:T(128)} %sub.14.count_ref, bf16[2048,2304]{1,0:T(8,128)(2,1)} %project.1.q_ref.k_ref.v_ref, bf16[2048,2304]{1,0:T(8,128)(2,1)} %project.1.q_ref.k_ref.v_ref, bf16[2048,2304]{1,0:T(8,128)(2,1)} %project.1.q_ref.k_ref.v_ref, ...), custom_call_target="tpu_custom_call" | custom-call | flops 625000000 | bytes 625000 | tf_op jit(solution)/shard_map/attend_backward/pallas_call | solution.py:226
  470.5 3.8 collective-permute-start.50
  474.5 7.2 %grad_qkv.5 = (bf16[192,768]{1,0:T(8,128)(2,1)}, bf16[192,768]{1,0:T(8,128)(2,1)}, bf16[384,768]{1,0:T(8,128)(2,1)}, f32[8,768]{1,0:T(8,128)}) custom-call(s32[8]{0:T(128)} %stack.247.owner_ref, bf16[2048,768]{1,0:T(8,128)(2,1)} %bitcast.105, bf16[2048,768]{1,0:T(8,128)(2,1)} %attend_backward.5.b_ref.refs_2_), custom_call_target="tpu_custom_call" | custom-call | flops 150994944 | bytes 466944 | tf_op jit(solution)/shard_map/grad_qkv/pallas_call | solution.py:503
  488.3 15.4 %input_grad.1 = bf16[2048,768]{1,0:T(8,128)(2,1)} custom-call(s32[6]{0:T(128)} %stack.238.starts_ref, bf16[2048,768]{1,0:T(8,128)(2,1)} %get-tuple-element.270.b_ref.dbranch_ref, bf16[2048,768]{1,0:T(8,128)(2,1)} %attend_backward.3.b_ref.refs_0_, bf16[2048,768]{1,0:T(8,128)(2,1)} %attend_backward.4.b_ref.refs_1_, ...), custom_call_target="tpu_custom_call" | custom-call | flops 452984832 | bytes 1204224 | tf_op jit(solution)/shard_map/input_grad/pallas_call | solution.py:455
  511.0 4.2 collective-permute-done.55
  540.3 3.2 collective-permute-done.67
  (371 shorter events, 135.4 us)
Async XLA Ops:
  27.8 29.3 %collective-permute-start.10 = (bf16[192,768]{1,0:T(8,128)(2,1)}, bf16[192,768]{1,0:T(8,128)(2,1)}, u32[]{:S(2)}, u32[]{:S(2)}) collective-permute-start(bf16[192,768]{1,0:T(8,128)(2,1)} %refs_0_.3), channel_id=1, source_target_pairs={{0,8},{8,0},{16,24},{24,16},{1,9},{9,1},{17,25},{25,17},{2,10},{10... | collective-permute-start | bytes 884744 | tf_op jit(solution)/shard_map/ppermute | solution.py:534
  28.1 40.5 %collective-permute-start.11 = (bf16[192,3072]{1,0:T(8,128)(2,1)}, bf16[192,3072]{1,0:T(8,128)(2,1)S(1)}, u32[]{:S(2)}, u32[]{:S(2)}) collective-permute-start(bf16[192,3072]{1,0:T(8,128)(2,1)} %refs_6_.1), channel_id=1, source_target_pairs={{0,8},{8,0},{16,24},{24,16},{1,9},{9,1},{17,25},{25,17},{2,10},{10... | collective-permute-start | bytes 3538952 | tf_op jit(solution)/shard_map/ppermute | solution.py:534
  28.4 40.1 %collective-permute-start.12 = (bf16[768,768]{1,0:T(8,128)(2,1)}, bf16[768,768]{1,0:T(8,128)(2,1)}, u32[]{:S(2)}, u32[]{:S(2)}) collective-permute-start(bf16[768,768]{1,0:T(8,128)(2,1)} %refs_12_.1), channel_id=1, source_target_pairs={{0,8},{8,0},{16,24},{24,16},{1,9},{9,1},{17,25},{25,17},{2,10},{10... | collective-permute-start | bytes 3538952 | tf_op jit(solution)/shard_map/ppermute | solution.py:534
  68.5 55.1 %collective-permute-start.17 = (bf16[96,3072]{1,0:T(8,128)(2,1)S(1)}, bf16[96,3072]{1,0:T(8,128)(2,1)S(1)}, u32[]{:S(2)}, u32[]{:S(2)}) collective-permute-start(bf16[96,3072]{1,0:T(8,128)(2,1)S(1)} %collective-permute-done.8.refs_8_), channel_id=1, source_target_pairs={{0,8},{8,0},{16,24},{24,16},{1,9},{9,1},{17,25},{25,17},{2,10},{10... | collective-permute-start | bytes 1769480 | tf_op jit(solution)/shard_map/ppermute | solution.py:534
  68.6 55.1 %collective-permute-start.14 = (bf16[96,3072]{1,0:T(8,128)(2,1)S(1)}, bf16[96,3072]{1,0:T(8,128)(2,1)S(1)}, u32[]{:S(2)}, u32[]{:S(2)}) collective-permute-start(bf16[96,3072]{1,0:T(8,128)(2,1)S(1)} %collective-permute-done.8.refs_8_), channel_id=1, source_target_pairs={{0,1},{1,0},{2,3},{3,2},{4,5},{5,4},{6,7},{7,6},{8,9},{9,8},{10,11... | collective-permute-start | bytes 1769480 | tf_op jit(solution)/shard_map/ppermute | solution.py:534
  70.2 53.5 %collective-permute-start.18 = (bf16[384,768]{1,0:T(8,128)(2,1)S(1)}, bf16[384,768]{1,0:T(8,128)(2,1)}, u32[]{:S(2)}, u32[]{:S(2)}) collective-permute-start(bf16[384,768]{1,0:T(8,128)(2,1)S(1)} %collective-permute-done.9.refs_14_), channel_id=1, source_target_pairs={{0,8},{8,0},{16,24},{24,16},{1,9},{9,1},{17,25},{25,17},{2,10},{10... | collective-permute-start | bytes 1769480 | tf_op jit(solution)/shard_map/ppermute | solution.py:534
  70.4 53.4 %collective-permute-start.15 = (bf16[384,768]{1,0:T(8,128)(2,1)S(1)}, bf16[384,768]{1,0:T(8,128)(2,1)}, u32[]{:S(2)}, u32[]{:S(2)}) collective-permute-start(bf16[384,768]{1,0:T(8,128)(2,1)S(1)} %collective-permute-done.9.refs_14_), channel_id=1, source_target_pairs={{0,1},{1,0},{2,3},{3,2},{4,5},{5,4},{6,7},{7,6},{8,9},{9,8},{10,11... | collective-permute-start | bytes 1769480 | tf_op jit(solution)/shard_map/ppermute | solution.py:534
  72.9 50.8 %collective-permute-start.13 = (bf16[96,768]{1,0:T(8,128)(2,1)}, bf16[96,768]{1,0:T(8,128)(2,1)}, u32[]{:S(2)}, u32[]{:S(2)}) collective-permute-start(bf16[96,768]{1,0:T(8,128)(2,1)} %collective-permute-done.7.refs_2_), channel_id=1, source_target_pairs={{0,1},{1,0},{2,3},{3,2},{4,5},{5,4},{6,7},{7,6},{8,9},{9,8},{10,11... | collective-permute-start | bytes 442376 | tf_op jit(solution)/shard_map/ppermute | solution.py:534
  206.5 40.4 %collective-permute-start.22 = (bf16[1536,768]{1,0:T(8,128)(2,1)}, bf16[1536,768]{1,0:T(8,128)(2,1)S(1)}, u32[]{:S(2)}, u32[]{:S(2)}) collective-permute-start(bf16[1536,768]{1,0:T(8,128)(2,1)} %get-tuple-element.222), channel_id=1, source_target_pairs={{0,8},{8,0},{16,24},{24,16},{1,9},{9,1},{17,25},{25,17},{2,10},{10... | collective-permute-start | bytes 7077896 | tf_op jit(solution)/shard_map/ppermute | solution.py:534
  263.0 31.3 %collective-permute-start.24 = (bf16[384,3072]{1,0:T(8,128)(2,1)}, bf16[384,3072]{1,0:T(8,128)(2,1)S(1)}, u32[]{:S(2)}, u32[]{:S(2)}) collective-permute-start(bf16[384,3072]{1,0:T(8,128)(2,1)} %get-tuple-element.232), channel_id=1, source_target_pairs={{0,8},{8,0},{16,24},{24,16},{1,9},{9,1},{17,25},{25,17},{2,10},{10... | collective-permute-start | bytes 7077896 | tf_op jit(solution)/shard_map/ppermute | solution.py:534
  296.1 41.7 %collective-permute-start.27 = (bf16[192,3072]{1,0:T(8,128)(2,1)}, bf16[192,3072]{1,0:T(8,128)(2,1)}, u32[]{:S(2)}, u32[]{:S(2)}) collective-permute-start(bf16[192,3072]{1,0:T(8,128)(2,1)} %add_convert_fusion.1), channel_id=1, source_target_pairs={{0,16},{8,24},{16,0},{24,8},{1,17},{9,25},{17,1},{25,9},{2,18},{10... | collective-permute-start | bytes 3538952 | tf_op jit(solution)/shard_map/ppermute | solution.py:534
  300.0 36.3 %collective-permute-start.26 = (bf16[384,768]{1,0:T(8,128)(2,1)S(1)}, bf16[384,768]{1,0:T(8,128)(2,1)S(1)}, u32[]{:S(2)}, u32[]{:S(2)}) collective-permute-start(bf16[384,768]{1,0:T(8,128)(2,1)S(1)} %constant_dynamic-slice_fusion.11), channel_id=1, source_target_pairs={{0,1},{1,0},{2,3},{3,2},{4,5},{5,4},{6,7},{7,6},{8,9},{9,8},{10,11... | collective-permute-start | bytes 1769480 | tf_op jit(solution)/shard_map/ppermute | solution.py:534
  300.9 35.4 %collective-permute-start.28 = (bf16[192,768]{1,0:T(8,128)(2,1)}, bf16[192,768]{1,0:T(8,128)(2,1)S(1)}, u32[]{:S(2)}, u32[]{:S(2)}) collective-permute-start(bf16[192,768]{1,0:T(8,128)(2,1)} %add_convert_fusion.17), channel_id=1, source_target_pairs={{0,16},{8,24},{16,0},{24,8},{1,17},{9,25},{17,1},{25,9},{2,18},{10... | collective-permute-start | bytes 884744 | tf_op jit(solution)/shard_map/ppermute | solution.py:534
  361.5 47.7 %collective-permute-start.34 = (bf16[48,3072]{1,0:T(8,128)(2,1)S(1)}, bf16[48,3072]{1,0:T(8,128)(2,1)S(1)}, u32[]{:S(2)}, u32[]{:S(2)}) collective-permute-start(bf16[48,3072]{1,0:T(8,128)(2,1)S(1)} %constant_dynamic-slice_fusion.7), channel_id=1, source_target_pairs={{0,2},{1,3},{2,0},{3,1},{4,6},{5,7},{6,4},{7,5},{8,10},{9,11},{10,... | collective-permute-start | bytes 884744 | tf_op jit(solution)/shard_map/ppermute | solution.py:534
  363.4 45.8 %collective-permute-start.33 = (bf16[192,768]{1,0:T(8,128)(2,1)S(1)}, bf16[192,768]{1,0:T(8,128)(2,1)S(1)}, u32[]{:S(2)}, u32[]{:S(2)}) collective-permute-start(bf16[192,768]{1,0:T(8,128)(2,1)S(1)} %add_convert_fusion.15), channel_id=1, source_target_pairs={{0,4},{1,5},{2,6},{3,7},{4,0},{5,1},{6,2},{7,3},{8,12},{9,13},{10,... | collective-permute-start | bytes 884744 | tf_op jit(solution)/shard_map/ppermute | solution.py:534
  366.7 42.6 %collective-permute-start.36 = (bf16[192,768]{1,0:T(8,128)(2,1)S(1)}, bf16[192,768]{1,0:T(8,128)(2,1)S(1)}, u32[]{:S(2)}, u32[]{:S(2)}) collective-permute-start(bf16[192,768]{1,0:T(8,128)(2,1)S(1)} %add_convert_fusion.14), channel_id=1, source_target_pairs={{0,16},{8,24},{16,0},{24,8},{1,17},{9,25},{17,1},{25,9},{2,18},{10... | collective-permute-start | bytes 884744 | tf_op jit(solution)/shard_map/ppermute | solution.py:534
  368.1 41.1 %collective-permute-start.35 = (bf16[48,768]{1,0:T(8,128)(2,1)S(1)}, bf16[48,768]{1,0:T(8,128)(2,1)S(1)}, u32[]{:S(2)}, u32[]{:S(2)}) collective-permute-start(bf16[48,768]{1,0:T(8,128)(2,1)S(1)} %constant_dynamic-slice_fusion.6), channel_id=1, source_target_pairs={{0,2},{1,3},{2,0},{3,1},{4,6},{5,7},{6,4},{7,5},{8,10},{9,11},{10,... | collective-permute-start | bytes 221192 | tf_op jit(solution)/shard_map/ppermute | solution.py:534
  428.4 40.6 %collective-permute-start.43 = (bf16[48,3072]{1,0:T(8,128)(2,1)S(1)}, bf16[48,3072]{1,0:T(8,128)(2,1)S(1)}, u32[]{:S(2)}, u32[]{:S(2)}) collective-permute-start(bf16[48,3072]{1,0:T(8,128)(2,1)S(1)} %add_convert_fusion.10), channel_id=1, source_target_pairs={{0,2},{1,3},{2,0},{3,1},{4,6},{5,7},{6,4},{7,5},{8,10},{9,11},{10,... | collective-permute-start | bytes 884744 | tf_op jit(solution)/shard_map/ppermute | solution.py:534
  429.2 39.8 %collective-permute-start.46 = (bf16[192,768]{1,0:T(8,128)(2,1)S(1)}, bf16[192,768]{1,0:T(8,128)(2,1)S(1)}, u32[]{:S(2)}, u32[]{:S(2)}) collective-permute-start(bf16[192,768]{1,0:T(8,128)(2,1)S(1)} %add_convert_fusion.9), channel_id=1, source_target_pairs={{0,16},{8,24},{16,0},{24,8},{1,17},{9,25},{17,1},{25,9},{2,18},{10... | collective-permute-start | bytes 884744 | tf_op jit(solution)/shard_map/ppermute | solution.py:534
  431.7 37.9 %collective-permute-start.42 = (bf16[384,768]{1,0:T(8,128)(2,1)S(1)}, bf16[384,768]{1,0:T(8,128)(2,1)S(1)}, u32[]{:S(2)}, u32[]{:S(2)}) collective-permute-start(bf16[384,768]{1,0:T(8,128)(2,1)S(1)} %bitcast.110), channel_id=1, source_target_pairs={{0,1},{1,0},{2,3},{3,2},{4,5},{5,4},{6,7},{7,6},{8,9},{9,8},{10,11... | collective-permute-start | bytes 1769480 | tf_op jit(solution)/shard_map/ppermute | solution.py:534
  432.1 36.8 %collective-permute-start.45 = (bf16[48,768]{1,0:T(8,128)(2,1)S(1)}, bf16[48,768]{1,0:T(8,128)(2,1)S(1)}, u32[]{:S(2)}, u32[]{:S(2)}) collective-permute-start(bf16[48,768]{1,0:T(8,128)(2,1)S(1)} %constant_dynamic-slice_fusion.4), channel_id=1, source_target_pairs={{0,2},{1,3},{2,0},{3,1},{4,6},{5,7},{6,4},{7,5},{8,10},{9,11},{10,... | collective-permute-start | bytes 221192 | tf_op jit(solution)/shard_map/ppermute | solution.py:534
  433.5 35.4 %collective-permute-start.44 = (bf16[48,768]{1,0:T(8,128)(2,1)S(1)}, bf16[48,768]{1,0:T(8,128)(2,1)S(1)}, u32[]{:S(2)}, u32[]{:S(2)}) collective-permute-start(bf16[48,768]{1,0:T(8,128)(2,1)S(1)} %add_convert_fusion.28), channel_id=1, source_target_pairs={{0,2},{1,3},{2,0},{3,1},{4,6},{5,7},{6,4},{7,5},{8,10},{9,11},{10,... | collective-permute-start | bytes 221192 | tf_op jit(solution)/shard_map/ppermute | solution.py:534
  469.7 34.0 %collective-permute-start.49 = (bf16[48,768]{1,0:T(8,128)(2,1)S(1)}, bf16[48,768]{1,0:T(8,128)(2,1)S(1)}, u32[]{:S(2)}, u32[]{:S(2)}) collective-permute-start(bf16[48,768]{1,0:T(8,128)(2,1)S(1)} %add_convert_fusion.27), channel_id=1, source_target_pairs={{0,4},{1,5},{2,6},{3,7},{4,0},{5,1},{6,2},{7,3},{8,12},{9,13},{10,... | collective-permute-start | bytes 221192 | tf_op jit(solution)/shard_map/ppermute | solution.py:534
  470.5 33.2 %collective-permute-start.50 = (bf16[96,768]{1,0:T(8,128)(2,1)}, bf16[96,768]{1,0:T(8,128)(2,1)}, u32[]{:S(2)}, u32[]{:S(2)}) collective-permute-start(bf16[96,768]{1,0:T(8,128)(2,1)} %constant_dynamic-slice_fusion.3), channel_id=1, source_target_pairs={{0,1},{1,0},{2,3},{3,2},{4,5},{5,4},{6,7},{7,6},{8,9},{9,8},{10,11... | collective-permute-start | bytes 442376 | tf_op jit(solution)/shard_map/ppermute | solution.py:534
  (97 other events, 1237.1 us)
